TPU v7x, 256 devices: a whole 4x4x8 slice. The times are simulated.
256 devices in a mesh: pair: 64 (over z, x, core), sp: 4 (over y).
Axes of the slice: x: 4, y: 4, z: 8, core: 2. Of those that a mesh axis runs over, the one named last changes fastest.
Arguments:
- gamma_pairs: bfloat16 [2, 64, 128, 30720], P(None, None, 'sp', 'pair'), may hold values from -6 to 6
- occ_coef: bfloat16 [30720, 128], P(None, 'sp'), may hold values from -0.5 to 0.5
- block_lists: int32 [4, 4, 20], replicated, may hold values from 0 to 79, as said below
- block_counts: int32 [4, 4], replicated, may hold values from 1 to 20, as said below
- block_coords: int32 [320, 2], replicated, may hold values from 0 to 239, as said below
Outputs:
- ao_gamma: bfloat16 [2, 64, 320, 128, 128], P(None, 'pair', 'sp')
Inputs may be any that keep to these rules, and one draw needn't show every extreme that they name: `block_lists`: the 20 entries of one list are distinct; entries past block_counts are not used. `block_counts`: in every draw some owner gets 20 blocks from every slab. `block_coords`: every one of the 240 column blocks is the column block of some shell-pair block.
All inputs are finite; a program needn't handle non-finite values.
Results may differ from a plain program's by a relative error of at most 0.0039.
Values may be sent and summed in bfloat16 or wider, within the bound.
No kernel may reach another device: no remote copies, remote signals or barrier semaphores. Data moves between devices by JAX's collectives and lax.ppermute only.
A program may use at most 128 MiB of HBM per device.

v0:
```python
import functools

import jax
import jax.numpy as jnp
from jax import lax
from jax.experimental import pallas as pl
from jax.experimental.pallas import tpu as pltpu
from jax.sharding import Mesh, PartitionSpec as P

BLK = 128
NZ, NX, NCORE = 8, 4, 2
LEVELS = (13, 30)
BF = jnp.bfloat16
VMEM = pl.BlockSpec(memory_space=pltpu.VMEM)
ANY = pl.BlockSpec(memory_space=pl.ANY)
SMEM = pl.BlockSpec(memory_space=pltpu.SMEM)


def params(mib):
    return pltpu.CompilerParams(vmem_limit_bytes=mib << 20)


def cost(nbytes, flops=0):
    return pl.CostEstimate(flops=flops, bytes_accessed=nbytes, transcendentals=0)


def turn(start, k, n):
    at = start + k
    at = jnp.where(at >= n, at - n, at)
    return jnp.where(at < 0, at + n, at)


def coef_pick_kernel(me, rows, coef, after, *outs):
    slots = outs[0].shape[0]
    for k, out in enumerate(outs):
        base = turn(me[0], k, len(outs)) * slots

        def step(t, _):
            start = pl.multiple_of(rows[base + t] * BLK, BLK)
            out[t] = coef[:, pl.ds(start, BLK)]
            return 0

        lax.fori_loop(0, slots, step, 0, unroll=4)


def coef_pick(me, coef_t, rows, after, groups):
    slots, occ = rows.shape[0] // groups, coef_t.shape[0]
    return pl.pallas_call(
        coef_pick_kernel,
        out_shape=[jax.ShapeDtypeStruct((slots, occ, BLK), BF)] * groups,
        in_specs=[SMEM, SMEM, VMEM, ANY],
        out_specs=[VMEM] * groups,
        compiler_params=params(16),
        cost_estimate=cost(4 << 20),
        name="coef_pick",
    )(me, rows, coef_t, after)


def coef_join_kernel(me, pos, *rest):
    pieces, out, held = rest[:-2], rest[-2], rest[-1]
    groups, owned = len(pieces), out.shape[0]
    for k, piece in enumerate(pieces):
        held[turn(me[0], -k, groups)] = piece[...]

    def step(k, _):
        parts = []
        for s in range(groups):
            p = pos[s * owned + k]
            block = held[s, jnp.maximum(p, 0)]
            parts.append(jnp.where(p >= 0, block, jnp.zeros_like(block)))
        out[k] = jnp.concatenate(parts, axis=0).T
        return 0

    lax.fori_loop(0, owned, step, 0, unroll=2)


def coef_join(me, pieces, pos, owned):
    groups = len(pieces)
    slots, occ, _ = pieces[0].shape
    return pl.pallas_call(
        coef_join_kernel,
        out_shape=jax.ShapeDtypeStruct((owned, BLK, groups * occ), BF),
        in_specs=[SMEM, SMEM] + [VMEM] * groups,
        out_specs=VMEM,
        scratch_shapes=[pltpu.VMEM((groups, slots, occ, BLK), BF)],
        compiler_params=params(16),
        cost_estimate=cost(4 << 20),
        name="coef_join",
    )(me, pos, *pieces)


def plane_split_kernel(batch, at, pairs, *rest):
    outs, sems = rest[:-1], rest[-1]
    copies = []
    for k, out in enumerate(outs):
        px = turn(at[0], k // NCORE, NX)
        pc = at[1] if k % NCORE == 0 else 1 - at[1]
        copies.append(pltpu.make_async_copy(pairs.at[batch, :, px, pc], out, sems.at[k]))
    for copy in copies:
        copy.start()
    for copy in copies:
        copy.wait()


def plane_split(batch, at, pairs):
    _, nz, nx, nc, occ, width = pairs.shape
    return pl.pallas_call(
        functools.partial(plane_split_kernel, batch),
        out_shape=[jax.ShapeDtypeStruct((nz, occ, width), BF)] * (nx * nc),
        in_specs=[SMEM, pl.BlockSpec(memory_space=pltpu.HBM)],
        out_specs=[VMEM] * (nx * nc),
        scratch_shapes=[pltpu.SemaphoreType.DMA((nx * nc,))],
        compiler_params=params(60),
        cost_estimate=cost(4 << 20),
        name=f"plane_split{batch}",
    )(at, pairs)


def plane_pick_kernel(at, listed, *rest):
    pieces, (out, got, tiles) = rest[:-3], rest[-3:]
    width = got.shape[3]
    blocks = tiles.shape[1]
    for k, piece in enumerate(pieces):
        sx = turn(at[0], -(k // NCORE), NX)
        sc = at[1] if k % NCORE == 0 else 1 - at[1]
        got[sx * NCORE + sc] = piece[...]

    def cut(pz, _):
        for j in range(blocks):
            src, off = divmod(j * BLK, width)
            if off + BLK <= width:
                tiles[pz, j] = got[src, pz, :, off : off + BLK]
            else:
                tiles[pz, j] = jnp.concatenate(
                    [got[src, pz, :, off:width], got[src + 1, pz, :, : off + BLK - width]], axis=1
                )
        return 0

    lax.fori_loop(0, NZ, cut, 0)

    def keep(j, _):
        block = listed[j]
        for pz in range(NZ):
            out[pz, j] = tiles[pz, block]
        return 0

    lax.fori_loop(0, out.shape[1], keep, 0)


def plane_pick(at, listed, pieces, cap):
    nz, occ, width = pieces[0].shape
    n = len(pieces)
    return pl.pallas_call(
        plane_pick_kernel,
        out_shape=jax.ShapeDtypeStruct((nz, cap, occ, BLK), BF),
        in_specs=[SMEM, SMEM] + [VMEM] * n,
        out_specs=VMEM,
        scratch_shapes=[
            pltpu.VMEM((n, nz, occ, width), BF),
            pltpu.VMEM((nz, n * width // BLK, occ, BLK), BF),
        ],
        compiler_params=params(24),
        cost_estimate=cost(4 << 20),
        name="plane_pick",
    )(at, listed, *pieces)


def slot_pick_kernel(me, plane, rank, got, *outs):
    slots = outs[0].shape[0]
    for k, out in enumerate(outs):
        base = turn(me[0], k, len(outs)) * slots

        def step(t, _):
            out[t] = got[plane[base + t], rank[base + t]]
            return 0

        lax.fori_loop(0, slots, step, 0, unroll=4)


def slot_pick(me, plane, rank, got, groups):
    slots = plane.shape[0] // groups
    occ = got.shape[2]
    return pl.pallas_call(
        slot_pick_kernel,
        out_shape=[jax.ShapeDtypeStruct((slots, occ, BLK), BF)] * groups,
        in_specs=[SMEM, SMEM, SMEM, VMEM],
        out_specs=[VMEM] * groups,
        compiler_params=params(16),
        cost_estimate=cost(2 << 20),
        name="slot_pick",
    )(me, plane, rank, got)


def product_kernel(per, groups, me, pos, coef, *rest):
    gamma, (out, held) = rest[:groups], rest[-2:]
    owned = pos.shape[0] // groups
    step = pl.program_id(0)

    @pl.when(step == 0)
    def _():
        for k in range(groups):
            held[turn(me[0], -k, groups)] = gamma[k][...]

    for j in range(per):
        at = [jnp.maximum(pos[s * owned + step * per + j], 0) for s in range(groups)]
        cols = jnp.concatenate([held[s, at[s]] for s in range(groups)], axis=0)
        total = jnp.dot(coef[j], cols, preferred_element_type=jnp.float32)
        out[0, 0, j] = total.astype(BF)


def product(batch, batches, me, coef, gamma, pos, prior):
    owned = coef.shape[0]
    groups = len(gamma)
    per = 20
    extra = [] if prior is None else [prior]
    return pl.pallas_call(
        functools.partial(product_kernel, per, groups),
        out_shape=jax.ShapeDtypeStruct((batches, 1, owned, BLK, BLK), BF),
        grid_spec=pltpu.PrefetchScalarGridSpec(
            num_scalar_prefetch=2,
            grid=(owned // per,),
            in_specs=[pl.BlockSpec((per, BLK, coef.shape[2]), lambda i, *_: (i, 0, 0))]
            + [pl.BlockSpec(gamma[0].shape, lambda i, *_: (0, 0, 0))] * groups
            + [ANY] * len(extra),
            out_specs=pl.BlockSpec((1, 1, per, BLK, BLK), lambda i, *_: (batch, 0, i, 0, 0)),
            scratch_shapes=[pltpu.VMEM((groups,) + gamma[0].shape, BF)],
        ),
        input_output_aliases={3 + groups: 0} if extra else {},
        compiler_params=params(16),
        cost_estimate=cost(6 << 20, 2 * owned * BLK**3),
        name=f"product{batch}",
    )(me, pos, coef, *gamma, *extra)


def local(gamma_pairs, occ_coef, block_lists, block_counts, block_coords):
    batches, aux, occ, width = gamma_pairs.shape
    groups = lax.axis_size("sp")
    basis = occ_coef.shape[0]
    nblk = basis // BLK
    per_plane = nblk // NZ
    plane_devs = NX * NCORE
    total_blocks = block_coords.shape[0]
    owned = total_blocks // groups
    capacity = block_lists.shape[2]
    me_s = lax.axis_index("sp")
    me_z = lax.axis_index("z")

    at = jnp.stack([lax.axis_index("x"), lax.axis_index("core")]).astype(jnp.int32)
    pairs = gamma_pairs.reshape(batches, NZ, NX, NCORE, occ, width)

    def exchange_plane(split):
        got = [split[0]]
        for k in range(1, plane_devs):
            dx, dc = divmod(k, NCORE)
            moves = [
                (x * NCORE + c, (x + dx) % NX * NCORE + (c ^ dc))
                for x in range(NX)
                for c in range(NCORE)
            ]
            got.append(lax.ppermute(split[k], ("x", "core"), moves))
        return got

    got0 = exchange_plane(plane_split(0, at, pairs))
    split1 = plane_split(1, at, pairs)

    valid = jnp.arange(capacity, dtype=jnp.int32)[None, None, :] < block_counts[:, :, None]
    lists = jnp.clip(block_lists, 0, owned - 1)
    ids = lists + (jnp.arange(groups, dtype=jnp.int32) * owned)[None, :, None]
    hit = ids.reshape(groups, -1, 1) == jnp.arange(total_blocks, dtype=jnp.int32)
    row_ids = jnp.sum(jnp.where(hit, block_coords[:, 0], 0), axis=2)
    col_ids = jnp.sum(jnp.where(hit, block_coords[:, 1], 0), axis=2)
    live_col = jnp.where(valid.reshape(groups, -1), col_ids, -1)
    need = jnp.any(live_col[:, :, None] == jnp.arange(nblk, dtype=jnp.int32), axis=1)
    need = need.reshape(groups, NZ, per_plane).astype(jnp.int32)
    most = jnp.max(jnp.sum(need, axis=2))
    my_need = lax.dynamic_index_in_dim(need, me_s, 0, keepdims=False)
    plane_ids = jnp.arange(per_plane, dtype=jnp.int32)
    before = (plane_ids[None, :] < plane_ids[:, None]).astype(jnp.int32)
    rank = jnp.sum(my_need[:, None, :] * before[None], axis=2)
    my_cols = lax.dynamic_index_in_dim(col_ids, me_s, 0, keepdims=False)
    my_rows = lax.dynamic_index_in_dim(row_ids, me_s, 0, keepdims=False)
    my_live = lax.dynamic_index_in_dim(valid.reshape(groups, -1), me_s, 0, keepdims=False)
    col_hit = my_cols[:, None] == jnp.arange(nblk, dtype=jnp.int32)
    slot_rank = jnp.sum(jnp.where(col_hit, rank.reshape(-1), 0), axis=1)
    slot_rank = jnp.where(my_live, slot_rank, 0)
    slot_plane = jnp.where(my_live, my_cols // per_plane, 0)
    plane_need = lax.dynamic_index_in_dim(my_need, me_z, 0, keepdims=False)
    plane_rank = lax.dynamic_index_in_dim(rank, me_z, 0, keepdims=False)
    listed = jnp.sum(
        jnp.where(
            (plane_rank[None, :] == plane_ids[:, None]) & (plane_need[None, :] > 0),
            plane_ids[None, :],
            0,
        ),
        axis=1,
    )
    to_me = lax.dynamic_index_in_dim(lists, me_s, 1, keepdims=False)
    to_me_valid = lax.dynamic_index_in_dim(valid, me_s, 1, keepdims=False)
    hits = (to_me[:, None, :] == jnp.arange(owned, dtype=jnp.int32)[None, :, None]) & to_me_valid[
        :, None, :
    ]
    slot_no = jnp.arange(capacity, dtype=jnp.int32) + 1
    pos = (jnp.sum(jnp.where(hits, slot_no, 0), axis=2) - 1).reshape(-1)

    me = me_s[None].astype(jnp.int32)
    def exchange_owners(sent):
        return [sent[0]] + [
            lax.ppermute(sent[k], "sp", [(i, (i + k) % groups) for i in range(groups)])
            for k in range(1, groups)
        ]

    def finish(cap, got0, split1, coef_t, my_rows, pos, listed, slot_plane, slot_rank):
        def planes(got):
            return lax.all_to_all(plane_pick(at, listed, got, cap), "z", 0, 0, tiled=True)

        def owners(got):
            return exchange_owners(slot_pick(me, slot_plane, slot_rank, got, groups))

        held0 = planes(got0)
        got1 = exchange_plane(split1)
        coef_parts = exchange_owners(coef_pick(me, coef_t, my_rows, got1[1], groups))
        coef = coef_join(me, coef_parts, pos, owned)
        held1 = planes(got1)
        out = product(0, batches, me, coef, owners(held0), pos, None)
        return product(1, batches, me, coef, owners(held1), pos, out)

    level = jnp.sum((most > jnp.array(LEVELS[:-1], jnp.int32)).astype(jnp.int32))
    level, my_rows, pos, listed, slot_plane, slot_rank = lax.optimization_barrier(
        (level, my_rows, pos, listed, slot_plane, slot_rank)
    )
    return lax.switch(
        level,
        [functools.partial(finish, cap) for cap in LEVELS],
        got0,
        split1,
        occ_coef.T,
        my_rows,
        pos,
        listed,
        slot_plane,
        slot_rank,
    )


def solution(mesh):
    groups = mesh.shape["sp"]
    grid = Mesh(mesh.devices.reshape(NZ, NX, NCORE, groups), ("z", "x", "core", "sp"))
    pair = ("z", "x", "core")
    in_specs = (P(None, None, "sp", pair), P(None, "sp"), P(), P(), P())
    out_specs = P(None, pair, "sp", None, None)
    return jax.shard_map(local, mesh=grid, in_specs=in_specs, out_specs=out_specs, check_vma=False)
```

profile of v0, /device:TPU:4, one launch (start us, length us, event | category | flops | bytes accessed | tf_op | source)
XLA Modules:
  0.0 124.4 jit_solution(7522578626858360021)
XLA Ops:
  0.1 3.3 %plane_split0.1 = (bf16[8,32,480]{2,1,0:T(8,128)(2,1)S(1)}, bf16[8,32,480]{2,1,0:T(8,128)(2,1)}, bf16[8,32,480]{2,1,0:T(8,128)(2,1)}, bf16[8,32,480]{2,1,0:T(8,1...) custom-call(s32[2]{0:T(128)S(1)} %pad_add_fusion.at, ...), custom_call_target="tpu_custom_call" | custom-call | bytes 4194304 | tf_op jit(solution)/shard_map/plane_split0/pallas_call | solution.py:107
  4.8 2.0 %collective-permute-start.34 = (bf16[8,32,480]{2,1,0:T(8,128)(2,1)}, bf16[8,32,480]{2,1,0:T(8,128)(2,1)S(1)}, u32[]{:S(2)}, u32[]{:S(2)}) collective-permute-start(bf16[8,32,480]{2,1,0:T(8,128)(2,1)} %get-tuple-element.215), channel_id=1, source_target_pairs={{0,12},{4,8},{8,20},{12,16},{16,28},{20,24},{24,4},{28,0},{1,13},{... | collective-permute-start | bytes 737288 | tf_op jit(solution)/shard_map/ppermute | solution.py:260
  6.9 3.1 %collective-permute-start.36 = (bf16[8,32,480]{2,1,0:T(8,128)(2,1)}, bf16[8,32,480]{2,1,0:T(8,128)(2,1)S(1)}, u32[]{:S(2)}, u32[]{:S(2)}) collective-permute-start(bf16[8,32,480]{2,1,0:T(8,128)(2,1)} %get-tuple-element.217), channel_id=1, source_target_pairs={{0,20},{4,16},{8,28},{12,24},{16,4},{20,0},{24,12},{28,8},{1,21},{... | collective-permute-start | bytes 737288 | tf_op jit(solution)/shard_map/ppermute | solution.py:260
  13.5 3.0 %plane_split1.1 = (bf16[8,32,480]{2,1,0:T(8,128)(2,1)S(1)}, bf16[8,32,480]{2,1,0:T(8,128)(2,1)S(1)}, bf16[8,32,480]{2,1,0:T(8,128)(2,1)S(1)}, bf16[8,32,480]{2,1...) custom-call(s32[2]{0:T(128)S(1)} %pad_add_fusion.at, ...), custom_call_target="tpu_custom_call" | custom-call | bytes 4194304 | tf_op jit(solution)/shard_map/plane_split1/pallas_call | solution.py:107
  18.0 6.5 %collective-permute-done.35 = bf16[8,32,480]{2,1,0:T(8,128)(2,1)S(1)} collective-permute-done((bf16[8,32,480]{2,1,0:T(8,128)(2,1)}, bf16[8,32,480]{2,1,0:T(8,128)(2,1)S(1)}, u32[]{:S(2)}, u32[]{:S(2)}) %collective-permute-start.35) | collective-permute-done | bytes 245792 | tf_op jit(solution)/shard_map/ppermute | solution.py:260
  24.5 5.1 %collective-permute-done.36 = bf16[8,32,480]{2,1,0:T(8,128)(2,1)S(1)} collective-permute-done((bf16[8,32,480]{2,1,0:T(8,128)(2,1)}, bf16[8,32,480]{2,1,0:T(8,128)(2,1)S(1)}, u32[]{:S(2)}, u32[]{:S(2)}) %collective-permute-start.36) | collective-permute-done | bytes 245792 | tf_op jit(solution)/shard_map/ppermute | solution.py:260
  29.5 2.2 %collective-permute-done.38 = bf16[8,32,480]{2,1,0:T(8,128)(2,1)S(1)} collective-permute-done((bf16[8,32,480]{2,1,0:T(8,128)(2,1)}, bf16[8,32,480]{2,1,0:T(8,128)(2,1)S(1)}, u32[]{:S(2)}, u32[]{:S(2)}) %collective-permute-start.38) | collective-permute-done | bytes 245792 | tf_op jit(solution)/shard_map/ppermute | solution.py:260
  31.7 92.7 %conditional.1 = (bf16[2,1,80,128,128]{4,3,2,1,0:T(8,128)(2,1)}) conditional(s32[]{:T(128)} %clamp.10, (bf16[8,32,480]{2,1,0:T(8,128)(2,1)S(1)}, s32[]{:T(128)}, s32[80]{0:T(128)S(1)}, bf16[32,30720]{1,0:T(8,128)(2,1)}, s32[320]{0:T(512)S(1)}, /*index=5*/bf16[8,32,480]{2,1,0:T(8,128)(2,1)S(1)}, bf16[8,32,480]{2,1,0:T(8,128)(2,1)S(1)}, ...), branch_computations={%region_9.10_spmd, %region_10.11_spmd} | conditional | flops 671088640 | bytes 59116828 | solution.py:331
  31.7 3.0 %plane_pick.5 = bf16[8,13,32,128]{3,2,1,0:T(8,128)(2,1)} custom-call(s32[2]{0:T(128)S(1)} %get-tuple-element.115.at, s32[30]{0:T(128)S(1)} %get-tuple-element.116.listed, bf16[8,32,480]{2,1,0:T(8,128)(2,1)S(1)} %get-tuple-element.128.rest_0_, bf16[8,32,480]{2,1,0:T(8,128)(2,1)S(1)} %get-tuple-element.129.rest_1_, ...), custom_call_target="tpu_custom_call" | custom-call | bytes 4194304 | tf_op jit(solution)/shard_map/cond/branch_0_fun/plane_pick/pallas_call | solution.py:153
  34.8 8.5 %all-to-all-start.1 = ((bf16[8,13,32,128]{3,2,1,0:T(8,128)(2,1)}), bf16[8,13,32,128]{3,2,1,0:T(8,128)(2,1)S(1)}, u32[]{:S(2)}, u32[]{:S(2)}) async-start(bf16[8,13,32,128]{3,2,1,0:T(8,128)(2,1)} %plane_pick.5), calls=%async_computation.1 | async-start | bytes 1703936 | tf_op jit(solution)/shard_map/cond/branch_0_fun/all_to_all | solution.py:314
  50.2 2.3 %collective-permute-done.4.rest_2_ = bf16[8,32,480]{2,1,0:T(8,128)(2,1)S(1)} collective-permute-done((bf16[8,32,480]{2,1,0:T(8,128)(2,1)S(1)}, bf16[8,32,480]{2,1,0:T(8,128)(2,1)S(1)}, u32[]{:S(2)}, u32[]{:S(2)}) %collective-permute-start.4) | collective-permute-done | bytes 245792 | tf_op jit(solution)/shard_map/cond/branch_0_fun/ppermute | solution.py:260
  53.2 4.3 %collective-permute-done.5.rest_3_ = bf16[8,32,480]{2,1,0:T(8,128)(2,1)S(1)} collective-permute-done((bf16[8,32,480]{2,1,0:T(8,128)(2,1)S(1)}, bf16[8,32,480]{2,1,0:T(8,128)(2,1)S(1)}, u32[]{:S(2)}, u32[]{:S(2)}) %collective-permute-start.5) | collective-permute-done | bytes 245792 | tf_op jit(solution)/shard_map/cond/branch_0_fun/ppermute | solution.py:260
  57.5 7.6 %collective-permute-done.6.rest_4_ = bf16[8,32,480]{2,1,0:T(8,128)(2,1)S(1)} collective-permute-done((bf16[8,32,480]{2,1,0:T(8,128)(2,1)S(1)}, bf16[8,32,480]{2,1,0:T(8,128)(2,1)S(1)}, u32[]{:S(2)}, u32[]{:S(2)}) %collective-permute-start.6) | collective-permute-done | bytes 245792 | tf_op jit(solution)/shard_map/cond/branch_0_fun/ppermute | solution.py:260
  65.1 4.7 %collective-permute-done.7.rest_5_ = bf16[8,32,480]{2,1,0:T(8,128)(2,1)S(1)} collective-permute-done((bf16[8,32,480]{2,1,0:T(8,128)(2,1)}, bf16[8,32,480]{2,1,0:T(8,128)(2,1)S(1)}, u32[]{:S(2)}, u32[]{:S(2)}) %collective-permute-start.7) | collective-permute-done | bytes 245792 | tf_op jit(solution)/shard_map/cond/branch_0_fun/ppermute | solution.py:260
  69.8 2.2 %collective-permute-done.9.rest_7_ = bf16[8,32,480]{2,1,0:T(8,128)(2,1)S(1)} collective-permute-done((bf16[8,32,480]{2,1,0:T(8,128)(2,1)}, bf16[8,32,480]{2,1,0:T(8,128)(2,1)S(1)}, u32[]{:S(2)}, u32[]{:S(2)}) %collective-permute-start.9) | collective-permute-done | bytes 245792 | tf_op jit(solution)/shard_map/cond/branch_0_fun/ppermute | solution.py:260
  71.9 3.0 %plane_pick.4 = bf16[8,13,32,128]{3,2,1,0:T(8,128)(2,1)} custom-call(s32[2]{0:T(128)S(1)} %get-tuple-element.115.at, s32[30]{0:T(128)S(1)} %get-tuple-element.116.listed, bf16[8,32,480]{2,1,0:T(8,128)(2,1)S(1)} %get-tuple-element.117.rest_0_, bf16[8,32,480]{2,1,0:T(8,128)(2,1)S(1)} %collective-permute-done.after.rest_1_, ...), custom_call_target="tpu_custom_call" | custom-call | bytes 4194304 | tf_op jit(solution)/shard_map/cond/branch_0_fun/plane_pick/pallas_call | solution.py:153
  75.0 7.0 %all-to-all-start = ((bf16[8,13,32,128]{3,2,1,0:T(8,128)(2,1)}), bf16[8,13,32,128]{3,2,1,0:T(8,128)(2,1)S(1)}, u32[]{:S(2)}, u32[]{:S(2)}) async-start(bf16[8,13,32,128]{3,2,1,0:T(8,128)(2,1)} %plane_pick.4), calls=%async_computation | async-start | bytes 1703936 | tf_op jit(solution)/shard_map/cond/branch_0_fun/all_to_all | solution.py:314
  85.7 2.9 %collective-permute-start.2 = (bf16[20,32,128]{2,1,0:T(8,128)(2,1)S(1)}, bf16[20,32,128]{2,1,0:T(8,128)(2,1)S(1)}, u32[]{:S(2)}, u32[]{:S(2)}) collective-permute-start(bf16[20,32,128]{2,1,0:T(8,128)(2,1)S(1)} %get-tuple-element.111), channel_id=1, source_target_pairs={{0,2},{1,3},{2,0},{3,1},{4,6},{5,7},{6,4},{7,5},{8,10},{9,11},{10,... | collective-permute-start | bytes 491528 | tf_op jit(solution)/shard_map/cond/branch_0_fun/ppermute | solution.py:308
  92.4 2.0 %collective-permute-start.15 = (bf16[20,32,128]{2,1,0:T(8,128)(2,1)S(1)}, bf16[20,32,128]{2,1,0:T(8,128)(2,1)S(1)}, u32[]{:S(2)}, u32[]{:S(2)}) collective-permute-start(bf16[20,32,128]{2,1,0:T(8,128)(2,1)S(1)} %get-tuple-element.139), channel_id=1, source_target_pairs={{0,3},{1,0},{2,1},{3,2},{4,7},{5,4},{6,5},{7,6},{8,11},{9,8},{10,9... | collective-permute-start | bytes 491528 | tf_op jit(solution)/shard_map/cond/branch_0_fun/ppermute | solution.py:308
  94.4 12.8 %all-to-all-done.got = bf16[8,13,32,128]{3,2,1,0:T(8,128)(2,1)S(1)} async-done(((bf16[8,13,32,128]{3,2,1,0:T(8,128)(2,1)}), bf16[8,13,32,128]{3,2,1,0:T(8,128)(2,1)S(1)}, u32[]{:S(2)}, u32[]{:S(2)}) %all-to-all-start) | async-done | bytes 852000 | tf_op jit(solution)/shard_map/cond/branch_0_fun/all_to_all | solution.py:314
  109.7 2.9 %collective-permute-start.11 = (bf16[20,32,128]{2,1,0:T(8,128)(2,1)S(1)}, bf16[20,32,128]{2,1,0:T(8,128)(2,1)S(1)}, u32[]{:S(2)}, u32[]{:S(2)}) collective-permute-start(bf16[20,32,128]{2,1,0:T(8,128)(2,1)S(1)} %get-tuple-element.126), channel_id=1, source_target_pairs={{0,2},{1,3},{2,0},{3,1},{4,6},{5,7},{6,4},{7,5},{8,10},{9,11},{10,... | collective-permute-start | bytes 491528 | tf_op jit(solution)/shard_map/cond/branch_0_fun/ppermute | solution.py:308
  114.0 3.7 %coef_join.2.coef = bf16[80,128,128]{2,1,0:T(8,128)(2,1)S(1)} custom-call(s32[1]{0:T(128)} %bitcast.me, s32[320]{0:T(512)S(1)} %get-tuple-element.105.pos, bf16[20,32,128]{2,1,0:T(8,128)(2,1)S(1)} %get-tuple-element.109.rest_0_, bf16[20,32,128]{2,1,0:T(8,128)(2,1)S(1)} %collective-permute-done.1.rest_1_, ...), custom_call_target="tpu_custom_call" | custom-call | bytes 4194304 | tf_op jit(solution)/shard_map/cond/branch_0_fun/coef_join/pallas_call | solution.py:80
  117.7 3.3 %product0.2.rest_4_ = bf16[2,1,80,128,128]{4,3,2,1,0:T(8,128)(2,1)} custom-call(s32[1]{0:T(128)} %bitcast.me, s32[320]{0:T(512)S(1)} %get-tuple-element.105.pos, bf16[80,128,128]{2,1,0:T(8,128)(2,1)S(1)} %coef_join.2.coef, bf16[20,32,128]{2,1,0:T(8,128)(2,1)S(1)} %get-tuple-element.136.rest_0_, bf16[20,32,128]{2,1,0:T(8,128)(2,1)S(1)} %collective-permute-done.13.rest_1_, ...), custom_call_target="tpu_custom_call" | custom-call | flops 335544320 | bytes 6291456 | tf_op jit(solution)/shard_map/cond/branch_0_fun/product0/pallas_call | solution.py:216
  121.1 3.3 %product1.2 = bf16[2,1,80,128,128]{4,3,2,1,0:T(8,128)(2,1)} custom-call(s32[1]{0:T(128)} %bitcast.me, s32[320]{0:T(512)S(1)} %get-tuple-element.105.pos, bf16[80,128,128]{2,1,0:T(8,128)(2,1)S(1)} %coef_join.2.coef, bf16[20,32,128]{2,1,0:T(8,128)(2,1)S(1)} %get-tuple-element.124.rest_0_, ...), custom_call_target="tpu_custom_call", output_to_operand_aliasing={{}: (7, {})} | custom-call | flops 335544320 | bytes 6291456 | tf_op jit(solution)/shard_map/cond/branch_0_fun/product1/pallas_call | solution.py:216
  (81 shorter events, 24.7 us)
Async XLA Ops:
  3.4 9.4 %collective-permute-start.32 = (bf16[8,32,480]{2,1,0:T(8,128)(2,1)}, bf16[8,32,480]{2,1,0:T(8,128)(2,1)S(1)}, u32[]{:S(2)}, u32[]{:S(2)}) collective-permute-start(bf16[8,32,480]{2,1,0:T(8,128)(2,1)} %get-tuple-element.213), channel_id=1, source_target_pairs={{0,4},{4,0},{8,12},{12,8},{16,20},{20,16},{24,28},{28,24},{1,5},{5... | collective-permute-start | bytes 737288 | tf_op jit(solution)/shard_map/ppermute | solution.py:260
  3.5 9.4 %collective-permute-start.33 = (bf16[8,32,480]{2,1,0:T(8,128)(2,1)}, bf16[8,32,480]{2,1,0:T(8,128)(2,1)S(1)}, u32[]{:S(2)}, u32[]{:S(2)}) collective-permute-start(bf16[8,32,480]{2,1,0:T(8,128)(2,1)} %get-tuple-element.214), channel_id=1, source_target_pairs={{0,8},{4,12},{8,16},{12,20},{16,24},{20,28},{24,0},{28,4},{1,9},{5... | collective-permute-start | bytes 737288 | tf_op jit(solution)/shard_map/ppermute | solution.py:260
  4.8 13.2 %collective-permute-start.34 = (bf16[8,32,480]{2,1,0:T(8,128)(2,1)}, bf16[8,32,480]{2,1,0:T(8,128)(2,1)S(1)}, u32[]{:S(2)}, u32[]{:S(2)}) collective-permute-start(bf16[8,32,480]{2,1,0:T(8,128)(2,1)} %get-tuple-element.215), channel_id=1, source_target_pairs={{0,12},{4,8},{8,20},{12,16},{16,28},{20,24},{24,4},{28,0},{1,13},{... | collective-permute-start | bytes 737288 | tf_op jit(solution)/shard_map/ppermute | solution.py:260
  6.8 17.7 %collective-permute-start.35 = (bf16[8,32,480]{2,1,0:T(8,128)(2,1)}, bf16[8,32,480]{2,1,0:T(8,128)(2,1)S(1)}, u32[]{:S(2)}, u32[]{:S(2)}) collective-permute-start(bf16[8,32,480]{2,1,0:T(8,128)(2,1)} %get-tuple-element.216), channel_id=1, source_target_pairs={{0,16},{4,20},{8,24},{12,28},{16,0},{20,4},{24,8},{28,12},{1,17},{... | collective-permute-start | bytes 737288 | tf_op jit(solution)/shard_map/ppermute | solution.py:260
  6.9 22.6 %collective-permute-start.36 = (bf16[8,32,480]{2,1,0:T(8,128)(2,1)}, bf16[8,32,480]{2,1,0:T(8,128)(2,1)S(1)}, u32[]{:S(2)}, u32[]{:S(2)}) collective-permute-start(bf16[8,32,480]{2,1,0:T(8,128)(2,1)} %get-tuple-element.217), channel_id=1, source_target_pairs={{0,20},{4,16},{8,28},{12,24},{16,4},{20,0},{24,12},{28,8},{1,21},{... | collective-permute-start | bytes 737288 | tf_op jit(solution)/shard_map/ppermute | solution.py:260
  12.9 16.6 %collective-permute-start.37 = (bf16[8,32,480]{2,1,0:T(8,128)(2,1)}, bf16[8,32,480]{2,1,0:T(8,128)(2,1)S(1)}, u32[]{:S(2)}, u32[]{:S(2)}) collective-permute-start(bf16[8,32,480]{2,1,0:T(8,128)(2,1)} %get-tuple-element.218), channel_id=1, source_target_pairs={{0,24},{4,28},{8,0},{12,4},{16,8},{20,12},{24,16},{28,20},{1,25},{... | collective-permute-start | bytes 737288 | tf_op jit(solution)/shard_map/ppermute | solution.py:260
  13.0 18.8 %collective-permute-start.38 = (bf16[8,32,480]{2,1,0:T(8,128)(2,1)}, bf16[8,32,480]{2,1,0:T(8,128)(2,1)S(1)}, u32[]{:S(2)}, u32[]{:S(2)}) collective-permute-start(bf16[8,32,480]{2,1,0:T(8,128)(2,1)} %get-tuple-element.219), channel_id=1, source_target_pairs={{0,28},{4,24},{8,4},{12,0},{16,12},{20,8},{24,20},{28,16},{1,29},{... | collective-permute-start | bytes 737288 | tf_op jit(solution)/shard_map/ppermute | solution.py:260
  34.8 40.2 %all-to-all-start.1 = ((bf16[8,13,32,128]{3,2,1,0:T(8,128)(2,1)}), bf16[8,13,32,128]{3,2,1,0:T(8,128)(2,1)S(1)}, u32[]{:S(2)}, u32[]{:S(2)}) async-start(bf16[8,13,32,128]{3,2,1,0:T(8,128)(2,1)} %plane_pick.5), calls=%async_computation.1 | async-start | bytes 1703936 | tf_op jit(solution)/shard_map/cond/branch_0_fun/all_to_all | solution.py:314
  43.4 9.1 %collective-permute-start.4 = (bf16[8,32,480]{2,1,0:T(8,128)(2,1)S(1)}, bf16[8,32,480]{2,1,0:T(8,128)(2,1)S(1)}, u32[]{:S(2)}, u32[]{:S(2)}) collective-permute-start(bf16[8,32,480]{2,1,0:T(8,128)(2,1)S(1)} %get-tuple-element.118), channel_id=1, source_target_pairs={{0,8},{4,12},{8,16},{12,20},{16,24},{20,28},{24,0},{28,4},{1,9},{5... | collective-permute-start | bytes 737288 | tf_op jit(solution)/shard_map/cond/branch_0_fun/ppermute | solution.py:260
  45.2 12.2 %collective-permute-start.5 = (bf16[8,32,480]{2,1,0:T(8,128)(2,1)S(1)}, bf16[8,32,480]{2,1,0:T(8,128)(2,1)S(1)}, u32[]{:S(2)}, u32[]{:S(2)}) collective-permute-start(bf16[8,32,480]{2,1,0:T(8,128)(2,1)S(1)} %get-tuple-element.119), channel_id=1, source_target_pairs={{0,12},{4,8},{8,20},{12,16},{16,28},{20,24},{24,4},{28,0},{1,13},{... | collective-permute-start | bytes 737288 | tf_op jit(solution)/shard_map/cond/branch_0_fun/ppermute | solution.py:260
  45.3 19.8 %collective-permute-start.6 = (bf16[8,32,480]{2,1,0:T(8,128)(2,1)S(1)}, bf16[8,32,480]{2,1,0:T(8,128)(2,1)S(1)}, u32[]{:S(2)}, u32[]{:S(2)}) collective-permute-start(bf16[8,32,480]{2,1,0:T(8,128)(2,1)S(1)} %get-tuple-element.120), channel_id=1, source_target_pairs={{0,16},{4,20},{8,24},{12,28},{16,0},{20,4},{24,8},{28,12},{1,17},{... | collective-permute-start | bytes 737288 | tf_op jit(solution)/shard_map/cond/branch_0_fun/ppermute | solution.py:260
  46.8 22.9 %collective-permute-start.7 = (bf16[8,32,480]{2,1,0:T(8,128)(2,1)}, bf16[8,32,480]{2,1,0:T(8,128)(2,1)S(1)}, u32[]{:S(2)}, u32[]{:S(2)}) collective-permute-start(bf16[8,32,480]{2,1,0:T(8,128)(2,1)} %get-tuple-element.121), channel_id=1, source_target_pairs={{0,20},{4,16},{8,28},{12,24},{16,4},{20,0},{24,12},{28,8},{1,21},{... | collective-permute-start | bytes 737288 | tf_op jit(solution)/shard_map/cond/branch_0_fun/ppermute | solution.py:260
  48.4 21.4 %collective-permute-start.8 = (bf16[8,32,480]{2,1,0:T(8,128)(2,1)}, bf16[8,32,480]{2,1,0:T(8,128)(2,1)S(1)}, u32[]{:S(2)}, u32[]{:S(2)}) collective-permute-start(bf16[8,32,480]{2,1,0:T(8,128)(2,1)} %get-tuple-element.122), channel_id=1, source_target_pairs={{0,24},{4,28},{8,0},{12,4},{16,8},{20,12},{24,16},{28,20},{1,25},{... | collective-permute-start | bytes 737288 | tf_op jit(solution)/shard_map/cond/branch_0_fun/ppermute | solution.py:260
  52.5 19.4 %collective-permute-start.9 = (bf16[8,32,480]{2,1,0:T(8,128)(2,1)}, bf16[8,32,480]{2,1,0:T(8,128)(2,1)S(1)}, u32[]{:S(2)}, u32[]{:S(2)}) collective-permute-start(bf16[8,32,480]{2,1,0:T(8,128)(2,1)} %get-tuple-element.123), channel_id=1, source_target_pairs={{0,28},{4,24},{8,4},{12,0},{16,12},{20,8},{24,20},{28,16},{1,29},{... | collective-permute-start | bytes 737288 | tf_op jit(solution)/shard_map/cond/branch_0_fun/ppermute | solution.py:260
  75.0 32.2 %all-to-all-start = ((bf16[8,13,32,128]{3,2,1,0:T(8,128)(2,1)}), bf16[8,13,32,128]{3,2,1,0:T(8,128)(2,1)S(1)}, u32[]{:S(2)}, u32[]{:S(2)}) async-start(bf16[8,13,32,128]{3,2,1,0:T(8,128)(2,1)} %plane_pick.4), calls=%async_computation | async-start | bytes 1703936 | tf_op jit(solution)/shard_map/cond/branch_0_fun/all_to_all | solution.py:314
  83.9 8.5 %collective-permute-start.1 = (bf16[20,32,128]{2,1,0:T(8,128)(2,1)S(1)}, bf16[20,32,128]{2,1,0:T(8,128)(2,1)S(1)}, u32[]{:S(2)}, u32[]{:S(2)}) collective-permute-start(bf16[20,32,128]{2,1,0:T(8,128)(2,1)S(1)} %get-tuple-element.110), channel_id=1, source_target_pairs={{0,1},{1,2},{2,3},{3,0},{4,5},{5,6},{6,7},{7,4},{8,9},{9,10},{10,1... | collective-permute-start | bytes 491528 | tf_op jit(solution)/shard_map/cond/branch_0_fun/ppermute | solution.py:308
  85.7 22.3 %collective-permute-start.2 = (bf16[20,32,128]{2,1,0:T(8,128)(2,1)S(1)}, bf16[20,32,128]{2,1,0:T(8,128)(2,1)S(1)}, u32[]{:S(2)}, u32[]{:S(2)}) collective-permute-start(bf16[20,32,128]{2,1,0:T(8,128)(2,1)S(1)} %get-tuple-element.111), channel_id=1, source_target_pairs={{0,2},{1,3},{2,0},{3,1},{4,6},{5,7},{6,4},{7,5},{8,10},{9,11},{10,... | collective-permute-start | bytes 491528 | tf_op jit(solution)/shard_map/cond/branch_0_fun/ppermute | solution.py:308
  88.6 21.1 %collective-permute-start.3 = (bf16[20,32,128]{2,1,0:T(8,128)(2,1)S(1)}, bf16[20,32,128]{2,1,0:T(8,128)(2,1)S(1)}, u32[]{:S(2)}, u32[]{:S(2)}) collective-permute-start(bf16[20,32,128]{2,1,0:T(8,128)(2,1)S(1)} %get-tuple-element.112), channel_id=1, source_target_pairs={{0,3},{1,0},{2,1},{3,2},{4,7},{5,4},{6,5},{7,6},{8,11},{9,8},{10,9... | collective-permute-start | bytes 491528 | tf_op jit(solution)/shard_map/cond/branch_0_fun/ppermute | solution.py:308
  90.8 21.8 %collective-permute-start.13 = (bf16[20,32,128]{2,1,0:T(8,128)(2,1)S(1)}, bf16[20,32,128]{2,1,0:T(8,128)(2,1)S(1)}, u32[]{:S(2)}, u32[]{:S(2)}) collective-permute-start(bf16[20,32,128]{2,1,0:T(8,128)(2,1)S(1)} %get-tuple-element.137), channel_id=1, source_target_pairs={{0,1},{1,2},{2,3},{3,0},{4,5},{5,6},{6,7},{7,4},{8,9},{9,10},{10,1... | collective-permute-start | bytes 491528 | tf_op jit(solution)/shard_map/cond/branch_0_fun/ppermute | solution.py:308
  91.6 26.1 %collective-permute-start.14 = (bf16[20,32,128]{2,1,0:T(8,128)(2,1)S(1)}, bf16[20,32,128]{2,1,0:T(8,128)(2,1)S(1)}, u32[]{:S(2)}, u32[]{:S(2)}) collective-permute-start(bf16[20,32,128]{2,1,0:T(8,128)(2,1)S(1)} %get-tuple-element.138), channel_id=1, source_target_pairs={{0,2},{1,3},{2,0},{3,1},{4,6},{5,7},{6,4},{7,5},{8,10},{9,11},{10,... | collective-permute-start | bytes 491528 | tf_op jit(solution)/shard_map/cond/branch_0_fun/ppermute | solution.py:308
  92.4 25.3 %collective-permute-start.15 = (bf16[20,32,128]{2,1,0:T(8,128)(2,1)S(1)}, bf16[20,32,128]{2,1,0:T(8,128)(2,1)S(1)}, u32[]{:S(2)}, u32[]{:S(2)}) collective-permute-start(bf16[20,32,128]{2,1,0:T(8,128)(2,1)S(1)} %get-tuple-element.139), channel_id=1, source_target_pairs={{0,3},{1,0},{2,1},{3,2},{4,7},{5,4},{6,5},{7,6},{8,11},{9,8},{10,9... | collective-permute-start | bytes 491528 | tf_op jit(solution)/shard_map/cond/branch_0_fun/ppermute | solution.py:308
  108.0 13.0 %collective-permute-start.10 = (bf16[20,32,128]{2,1,0:T(8,128)(2,1)S(1)}, bf16[20,32,128]{2,1,0:T(8,128)(2,1)S(1)}, u32[]{:S(2)}, u32[]{:S(2)}) collective-permute-start(bf16[20,32,128]{2,1,0:T(8,128)(2,1)S(1)} %get-tuple-element.125), channel_id=1, source_target_pairs={{0,1},{1,2},{2,3},{3,0},{4,5},{5,6},{6,7},{7,4},{8,9},{9,10},{10,1... | collective-permute-start | bytes 491528 | tf_op jit(solution)/shard_map/cond/branch_0_fun/ppermute | solution.py:308
  109.7 11.3 %collective-permute-start.11 = (bf16[20,32,128]{2,1,0:T(8,128)(2,1)S(1)}, bf16[20,32,128]{2,1,0:T(8,128)(2,1)S(1)}, u32[]{:S(2)}, u32[]{:S(2)}) collective-permute-start(bf16[20,32,128]{2,1,0:T(8,128)(2,1)S(1)} %get-tuple-element.126), channel_id=1, source_target_pairs={{0,2},{1,3},{2,0},{3,1},{4,6},{5,7},{6,4},{7,5},{8,10},{9,11},{10,... | collective-permute-start | bytes 491528 | tf_op jit(solution)/shard_map/cond/branch_0_fun/ppermute | solution.py:308
  112.6 8.4 %collective-permute-start.12 = (bf16[20,32,128]{2,1,0:T(8,128)(2,1)S(1)}, bf16[20,32,128]{2,1,0:T(8,128)(2,1)S(1)}, u32[]{:S(2)}, u32[]{:S(2)}) collective-permute-start(bf16[20,32,128]{2,1,0:T(8,128)(2,1)S(1)} %get-tuple-element.127), channel_id=1, source_target_pairs={{0,3},{1,0},{2,1},{3,2},{4,7},{5,4},{6,5},{7,6},{8,11},{9,8},{10,9... | collective-permute-start | bytes 491528 | tf_op jit(solution)/shard_map/cond/branch_0_fun/ppermute | solution.py:308
  (4 other events, 35.7 us)
where the time goes:
time: 126 us; the launch traced here: 124 us
  waiting for transfers between devices  47.7 us (38%)
  starting transfers between devices  45.7 us (36%)
  Pallas kernels  26.4 us (21%)
  other arithmetic  2.56 us (2%)
    ppermute x14, waiting for transfers between devices, exchange_plane(): got.append(lax.ppermute(split[k], ('x', 'core'), moves))  34.8 us
    ppermute x9, starting transfers between devices, exchange_owners(): lax.ppermute(sent[k], 'sp', [(i, (i + k) % groups) for i in range(groups)])  15.5 us
    all_to_all x2, starting transfers between devices, planes(): lax.all_to_all(plane_pick(at, listed, got, cap), 'z', 0, 0, tiled=True)  15.5 us
    ppermute x14, starting transfers between devices, exchange_plane(): got.append(lax.ppermute(split[k], ('x', 'core'), moves))  14.7 us
    all_to_all x2, waiting for transfers between devices, planes(): lax.all_to_all(plane_pick(at, listed, got, cap), 'z', 0, 0, tiled=True)  12.8 us
    pallas_call x2, Pallas kernels, product(): pl.pallas_call(functools.partial(product_kernel, per, groups), out_shape=...  6.65 us
    pallas_call x2, Pallas kernels, plane_split(): pl.pallas_call(functools.partial(plane_split_kernel, batch), out_shape=[j...  6.38 us
    pallas_call x2, Pallas kernels, plane_pick(): pl.pallas_call(plane_pick_kernel, out_shape=jax.ShapeDtypeStruct((nz, cap...  6.06 us
  transfers between devices with their start and end apart: 25, of which 9 were waited for; matrix products, arithmetic and copies ran while one was open for 3% of the time, Pallas kernels for 13%

commit v1 on v0

--- a/solution.py
+++ b/solution.py
@@ -9,7 +9,8 @@
 
 BLK = 128
 NZ, NX, NCORE = 8, 4, 2
-LEVELS = (13, 30)
+CAP = 13
+AFTER = 5
 BF = jnp.bfloat16
 VMEM = pl.BlockSpec(memory_space=pltpu.VMEM)
 ANY = pl.BlockSpec(memory_space=pl.ANY)
@@ -110,20 +111,41 @@
         in_specs=[SMEM, pl.BlockSpec(memory_space=pltpu.HBM)],
         out_specs=[VMEM] * (nx * nc),
         scratch_shapes=[pltpu.SemaphoreType.DMA((nx * nc,))],
-        compiler_params=params(60),
+        compiler_params=params(8),
         cost_estimate=cost(4 << 20),
         name=f"plane_split{batch}",
     )(at, pairs)
 
 
-def plane_pick_kernel(at, listed, *rest):
-    pieces, (out, got, tiles) = rest[:-3], rest[-3:]
+def plane_pack_kernel(batch, pairs, *rest):
+    out, sems = rest[-2:]
+    copies = [
+        pltpu.make_async_copy(pairs.at[batch, :, k // NCORE, k % NCORE], out.at[k], sems.at[k])
+        for k in range(NX * NCORE)
+    ]
+    for copy in copies:
+        copy.start()
+    for copy in copies:
+        copy.wait()
+
+
+def plane_pack(batch, pairs, after):
+    _, nz, nx, nc, occ, width = pairs.shape
+    return pl.pallas_call(
+        functools.partial(plane_pack_kernel, batch),
+        out_shape=jax.ShapeDtypeStruct((nx * nc, nz, occ, width), BF),
+        in_specs=[pl.BlockSpec(memory_space=pltpu.HBM)] + [ANY] * len(after),
+        out_specs=VMEM,
+        scratch_shapes=[pltpu.SemaphoreType.DMA((nx * nc,))],
+        compiler_params=params(8),
+        cost_estimate=cost(4 << 20),
+        name="plane_pack",
+    )(pairs, *after)
+
+
+def listed_tiles(out_of, count, listed, got, tiles):
     width = got.shape[3]
     blocks = tiles.shape[1]
-    for k, piece in enumerate(pieces):
-        sx = turn(at[0], -(k // NCORE), NX)
-        sc = at[1] if k % NCORE == 0 else 1 - at[1]
-        got[sx * NCORE + sc] = piece[...]
 
     def cut(pz, _):
         for j in range(blocks):
@@ -140,32 +162,72 @@
 
     def keep(j, _):
         block = listed[j]
-        for pz in range(NZ):
-            out[pz, j] = tiles[pz, block]
+        for k in range(NZ):
+            out_of(k, j, block)
         return 0
 
-    lax.fori_loop(0, out.shape[1], keep, 0)
-
-
-def plane_pick(at, listed, pieces, cap):
+    lax.fori_loop(0, count, keep, 0)
+
+
+def plane_pick_turned_kernel(at, listed, *rest):
+    pieces, outs, (got, tiles) = rest[: NX * NCORE], rest[NX * NCORE : -2], rest[-2:]
+    for k, piece in enumerate(pieces):
+        sx = turn(at[0], -(k // NCORE), NX)
+        sc = at[1] if k % NCORE == 0 else 1 - at[1]
+        got[sx * NCORE + sc] = piece[...]
+
+    def put(k, j, block):
+        outs[k][j] = tiles[turn(at[2], k, NZ), block]
+
+    listed_tiles(put, outs[0].shape[0], listed, got, tiles)
+
+
+def plane_pick_turned(at, listed, pieces, cap):
     nz, occ, width = pieces[0].shape
     n = len(pieces)
     return pl.pallas_call(
-        plane_pick_kernel,
-        out_shape=jax.ShapeDtypeStruct((nz, cap, occ, BLK), BF),
+        plane_pick_turned_kernel,
+        out_shape=[jax.ShapeDtypeStruct((cap, occ, BLK), BF)] * nz,
         in_specs=[SMEM, SMEM] + [VMEM] * n,
-        out_specs=VMEM,
+        out_specs=[VMEM] * nz,
         scratch_shapes=[
             pltpu.VMEM((n, nz, occ, width), BF),
             pltpu.VMEM((nz, n * width // BLK, occ, BLK), BF),
         ],
         compiler_params=params(24),
         cost_estimate=cost(4 << 20),
+        name="plane_pick_turned",
+    )(at, listed, *pieces)
+
+
+def plane_pick_kernel(listed, got, after, out, tiles):
+    def put(k, j, block):
+        out[k, j] = tiles[k, block]
+
+    listed_tiles(put, out.shape[1], listed, got, tiles)
+
+
+def plane_pick(listed, got, cap, after):
+    n, nz, occ, width = got.shape
+    return pl.pallas_call(
+        plane_pick_kernel,
+        out_shape=jax.ShapeDtypeStruct((nz, cap, occ, BLK), BF),
+        in_specs=[SMEM, VMEM, ANY],
+        out_specs=VMEM,
+        scratch_shapes=[pltpu.VMEM((nz, n * width // BLK, occ, BLK), BF)],
+        compiler_params=params(20),
+        cost_estimate=cost(4 << 20),
         name="plane_pick",
-    )(at, listed, *pieces)
-
-
-def slot_pick_kernel(me, plane, rank, got, *outs):
+    )(listed, got, after)
+
+
+def slot_pick_kernel(me, plane, rank, after, *rest):
+    if len(rest) <= NZ:
+        got, outs = rest[0], rest[1:]
+    else:
+        pieces, outs, got = rest[:NZ], rest[NZ:-1], rest[-1]
+        for k, piece in enumerate(pieces):
+            got[turn(me[1], -k, NZ)] = piece[...]
     slots = outs[0].shape[0]
     for k, out in enumerate(outs):
         base = turn(me[0], k, len(outs)) * slots
@@ -177,18 +239,21 @@
         lax.fori_loop(0, slots, step, 0, unroll=4)
 
 
-def slot_pick(me, plane, rank, got, groups):
+def slot_pick(me, plane, rank, got, after, groups):
+    pieces = got if isinstance(got, list) else [got]
     slots = plane.shape[0] // groups
-    occ = got.shape[2]
+    cap, occ, _ = pieces[0].shape[-3:]
+    turned = len(pieces) > 1
     return pl.pallas_call(
         slot_pick_kernel,
         out_shape=[jax.ShapeDtypeStruct((slots, occ, BLK), BF)] * groups,
-        in_specs=[SMEM, SMEM, SMEM, VMEM],
+        in_specs=[SMEM, SMEM, SMEM, ANY] + [VMEM] * len(pieces),
         out_specs=[VMEM] * groups,
+        scratch_shapes=[pltpu.VMEM((NZ, cap, occ, BLK), BF)] if turned else [],
         compiler_params=params(16),
         cost_estimate=cost(2 << 20),
         name="slot_pick",
-    )(me, plane, rank, got)
+    )(me, plane, rank, after, *pieces)
 
 
 def product_kernel(per, groups, me, pos, coef, *rest):
@@ -245,8 +310,9 @@
     me_s = lax.axis_index("sp")
     me_z = lax.axis_index("z")
 
-    at = jnp.stack([lax.axis_index("x"), lax.axis_index("core")]).astype(jnp.int32)
+    at = jnp.stack([lax.axis_index(name) for name in ("x", "core", "z")]).astype(jnp.int32)
     pairs = gamma_pairs.reshape(batches, NZ, NX, NCORE, occ, width)
+    pairs = pltpu.with_memory_space_constraint(pairs, pltpu.HBM)
 
     def exchange_plane(split):
         got = [split[0]]
@@ -261,7 +327,7 @@
         return got
 
     got0 = exchange_plane(plane_split(0, at, pairs))
-    split1 = plane_split(1, at, pairs)
+    got1 = lax.all_to_all(plane_pack(1, pairs, got0[1 : 1 + AFTER]), ("x", "core"), 0, 0, tiled=True)
 
     valid = jnp.arange(capacity, dtype=jnp.int32)[None, None, :] < block_counts[:, :, None]
     lists = jnp.clip(block_lists, 0, owned - 1)
@@ -302,44 +368,43 @@
     slot_no = jnp.arange(capacity, dtype=jnp.int32) + 1
     pos = (jnp.sum(jnp.where(hits, slot_no, 0), axis=2) - 1).reshape(-1)
 
-    me = me_s[None].astype(jnp.int32)
+    me = jnp.stack([me_s, me_z]).astype(jnp.int32)
     def exchange_owners(sent):
         return [sent[0]] + [
             lax.ppermute(sent[k], "sp", [(i, (i + k) % groups) for i in range(groups)])
             for k in range(1, groups)
         ]
 
-    def finish(cap, got0, split1, coef_t, my_rows, pos, listed, slot_plane, slot_rank):
-        def planes(got):
-            return lax.all_to_all(plane_pick(at, listed, got, cap), "z", 0, 0, tiled=True)
-
-        def owners(got):
-            return exchange_owners(slot_pick(me, slot_plane, slot_rank, got, groups))
-
-        held0 = planes(got0)
-        got1 = exchange_plane(split1)
-        coef_parts = exchange_owners(coef_pick(me, coef_t, my_rows, got1[1], groups))
-        coef = coef_join(me, coef_parts, pos, owned)
-        held1 = planes(got1)
-        out = product(0, batches, me, coef, owners(held0), pos, None)
-        return product(1, batches, me, coef, owners(held1), pos, out)
-
-    level = jnp.sum((most > jnp.array(LEVELS[:-1], jnp.int32)).astype(jnp.int32))
-    level, my_rows, pos, listed, slot_plane, slot_rank = lax.optimization_barrier(
-        (level, my_rows, pos, listed, slot_plane, slot_rank)
-    )
-    return lax.switch(
-        level,
-        [functools.partial(finish, cap) for cap in LEVELS],
-        got0,
-        split1,
-        occ_coef.T,
-        my_rows,
-        pos,
-        listed,
-        slot_plane,
-        slot_rank,
-    )
+    listed = listed[:CAP]
+    slot_at = jnp.minimum(slot_rank, CAP - 1)
+
+    sent0 = plane_pick_turned(at, listed, got0, CAP)
+    held0 = [sent0[0]] + [
+        lax.ppermute(sent0[k], "z", [(i, (i + k) % NZ) for i in range(NZ)]) for k in range(1, NZ)
+    ]
+    parts0 = slot_pick(me, slot_plane, slot_at, held0, me, groups)
+    coef_parts = exchange_owners(coef_pick(me, occ_coef.T, my_rows, parts0[0], groups))
+    coef = coef_join(me, coef_parts, pos, owned)
+    held1 = lax.all_to_all(plane_pick(listed, got1, CAP, parts0[0]), "z", 0, 0, tiled=True)
+    out = product(0, batches, me, coef, exchange_owners(parts0), pos, None)
+    parts1 = slot_pick(me, slot_plane, slot_at, held1, out[0, 0, 0, :8], groups)
+    out = product(1, batches, me, coef, exchange_owners(parts1), pos, out)
+
+    def all_columns(out):
+        gathered = lax.all_to_all(gamma_pairs, ("z", "x", "core"), 1, 3, tiled=True)
+        blocks = gathered.reshape(batches, occ, nblk, BLK)
+        taken = jnp.take(blocks, my_cols, axis=2).transpose(0, 2, 1, 3)
+        for b in range(batches):
+            sent = taken[b].reshape(groups, capacity, occ, BLK)
+            gamma = lax.all_to_all(sent, "sp", 0, 0, tiled=True)
+            parts = [
+                lax.dynamic_index_in_dim(gamma, (me_s - k + groups) % groups, 0, keepdims=False)
+                for k in range(groups)
+            ]
+            out = product(b, batches, me, coef, parts, pos, out)
+        return out
+
+    return lax.cond(most > CAP, all_columns, lambda out: out, out)
 
 
 def solution(mesh):

time: 126 us -> 127 us (level); the launches traced: 124 us -> 127 us
  waiting for transfers between devices: 47.7 us -> 38.2 us
  starting transfers between devices: 45.7 us -> 52.9 us
  local copies, waits for them, and re-layouts: 1.19 us -> 8.06 us
  Pallas kernels: 26.4 us -> 24.1 us
    ppermute x0 -> x7, starting transfers between devices: none -> 19.5 us  [local(): lax.ppermute(sent0[k], 'z', [(i, (i + k) % NZ) for i in range(NZ)])]
    ppermute x14 -> x7, waiting for transfers between devices: 34.8 us -> 19.3 us  [exchange_plane(): got.append(lax.ppermute(split[k], ('x', 'core'), moves))]
    all_to_all x2, waiting for transfers between devices: 12.8 us -> 0.01 us  [the longest x1 0.01 us: local(): lax.all_to_all(plane_pack(1, pairs, got0[1:1 + AFTER]), ('x', 'core'), 0,...]
    ppermute x0 -> x7, waiting for transfers between devices: none -> 10.3 us  [local(): lax.ppermute(sent0[k], 'z', [(i, (i + k) % NZ) for i in range(NZ)])]
    ppermute x9, waiting for transfers between devices: 0.02 us -> 8.66 us  [exchange_owners(): lax.ppermute(sent[k], 'sp', [(i, (i + k) % groups) for i in range(groups)])]
    ppermute x14 -> x7, starting transfers between devices: 14.7 us -> 6.6 us  [exchange_plane(): got.append(lax.ppermute(split[k], ('x', 'core'), moves))]
    unnamed x7 -> x21, local copies, waits for them, and re-layouts: 0.1 us -> 6.96 us
    pallas_call x0 -> x2, Pallas kernels: none -> 4.48 us  [the longest x1 2.9 us: plane_pick_turned(): pl.pallas_call(plane_pick_turned_kernel, out_shape=[jax.ShapeDtypeStruct(...]
  transfers between devices with their start and end apart: 25 -> 25, of which waited for: 9 -> 13; matrix products, arithmetic and copies ran while one was open for 3% -> 3% of each run, Pallas kernels for 13% -> 9%
where the time goes in v1:
time: 127 us
  starting transfers between devices  52.9 us (42%)
  waiting for transfers between devices  38.2 us (30%)
  Pallas kernels  24.1 us (19%)
  local copies, waits for them, and re-layouts  8.06 us (6%)
  other arithmetic  2.65 us (2%)
    ppermute x7, starting transfers between devices, local(): lax.ppermute(sent0[k], 'z', [(i, (i + k) % NZ) for i in range(NZ)])  19.5 us
    ppermute x7, waiting for transfers between devices, exchange_plane(): got.append(lax.ppermute(split[k], ('x', 'core'), moves))  19.3 us
    ppermute x9, starting transfers between devices, exchange_owners(): lax.ppermute(sent[k], 'sp', [(i, (i + k) % groups) for i in range(groups)])  15.5 us
    ppermute x7, waiting for transfers between devices, local(): lax.ppermute(sent0[k], 'z', [(i, (i + k) % NZ) for i in range(NZ)])  10.3 us
    ppermute x9, waiting for transfers between devices, exchange_owners(): lax.ppermute(sent[k], 'sp', [(i, (i + k) % groups) for i in range(groups)])  8.66 us
    pallas_call x2, Pallas kernels, product(): pl.pallas_call(functools.partial(product_kernel, per, groups), out_shape=...  7.46 us
    unnamed x21, local copies, waits for them, and re-layouts  6.96 us
    ppermute x7, starting transfers between devices, exchange_plane(): got.append(lax.ppermute(split[k], ('x', 'core'), moves))  6.6 us
  transfers between devices with their start and end apart: 25, of which 13 were waited for; matrix products, arithmetic and copies ran while one was open for 3% of the time, Pallas kernels for 9%

profile of v1, /device:TPU:4, one launch (start us, length us, event | category | flops | bytes accessed | tf_op | source)
XLA Modules:
  0.0 126.9 jit_solution(15769383899607187439)
XLA Ops:
  0.1 2.9 %plane_split0.1 = (bf16[8,32,480]{2,1,0:T(8,128)(2,1)S(1)}, bf16[8,32,480]{2,1,0:T(8,128)(2,1)S(1)}, bf16[8,32,480]{2,1,0:T(8,128)(2,1)S(1)}, bf16[8,32,480]{2,1...) custom-call(s32[3]{0:T(128)S(1)} %pad_add_fusion.1.at, ...), custom_call_target="tpu_custom_call" | custom-call | bytes 4194304 | tf_op jit(solution)/shard_map/plane_split0/pallas_call | solution.py:108
  7.0 3.1 %collective-permute-start.4 = (bf16[8,32,480]{2,1,0:T(8,128)(2,1)S(1)}, bf16[8,32,480]{2,1,0:T(8,128)(2,1)S(1)}, u32[]{:S(2)}, u32[]{:S(2)}) collective-permute-start(bf16[8,32,480]{2,1,0:T(8,128)(2,1)S(1)} %get-tuple-element.63), channel_id=1, source_target_pairs={{0,20},{4,16},{8,28},{12,24},{16,4},{20,0},{24,12},{28,8},{1,21},{... | collective-permute-start | bytes 737288 | tf_op jit(solution)/shard_map/ppermute | solution.py:326
  10.1 2.7 %collective-permute-done.1.rest_2_.rest_1_ = bf16[8,32,480]{2,1,0:T(8,128)(2,1)S(1)} collective-permute-done((bf16[8,32,480]{2,1,0:T(8,128)(2,1)S(1)}, bf16[8,32,480]{2,1,0:T(8,128)(2,1)S(1)}, u32[]{:S(2)}, u32[]{:S(2)}) %collective-permute-start.1) | collective-permute-done | bytes 245792 | tf_op jit(solution)/shard_map/ppermute | solution.py:326
  13.0 4.6 %collective-permute-done.2.rest_3_.rest_2_ = bf16[8,32,480]{2,1,0:T(8,128)(2,1)S(1)} collective-permute-done((bf16[8,32,480]{2,1,0:T(8,128)(2,1)S(1)}, bf16[8,32,480]{2,1,0:T(8,128)(2,1)S(1)}, u32[]{:S(2)}, u32[]{:S(2)}) %collective-permute-start.2) | collective-permute-done | bytes 245792 | tf_op jit(solution)/shard_map/ppermute | solution.py:326
  17.7 6.7 %collective-permute-done.3.rest_4_.rest_3_ = bf16[8,32,480]{2,1,0:T(8,128)(2,1)S(1)} collective-permute-done((bf16[8,32,480]{2,1,0:T(8,128)(2,1)S(1)}, bf16[8,32,480]{2,1,0:T(8,128)(2,1)S(1)}, u32[]{:S(2)}, u32[]{:S(2)}) %collective-permute-start.3) | collective-permute-done | bytes 245792 | tf_op jit(solution)/shard_map/ppermute | solution.py:326
  24.4 5.2 %collective-permute-done.4.rest_5_.rest_4_ = bf16[8,32,480]{2,1,0:T(8,128)(2,1)S(1)} collective-permute-done((bf16[8,32,480]{2,1,0:T(8,128)(2,1)S(1)}, bf16[8,32,480]{2,1,0:T(8,128)(2,1)S(1)}, u32[]{:S(2)}, u32[]{:S(2)}) %collective-permute-start.4) | collective-permute-done | bytes 245792 | tf_op jit(solution)/shard_map/ppermute | solution.py:326
  32.5 6.4 %all-to-all-start.3 = ((bf16[8,8,32,480]{3,2,1,0:T(8,128)(2,1)}), bf16[8,8,32,480]{3,2,1,0:T(8,128)(2,1)S(1)}, u32[]{:S(2)}, u32[]{:S(2)}) async-start(bf16[8,8,32,480]{3,2,1,0:T(8,128)(2,1)} %copy-done), calls=%async_computation.3 | async-start | bytes 4194304 | tf_op jit(solution)/shard_map/all_to_all | solution.py:330
  42.2 2.9 %plane_pick_turned.1 = (bf16[13,32,128]{2,1,0:T(8,128)(2,1)S(1)}, bf16[13,32,128]{2,1,0:T(8,128)(2,1)S(1)}, bf16[13,32,128]{2,1,0:T(8,128)(2,1)S(1)}, bf16[13,32...) custom-call(s32[3]{0:T(128)S(1)} %pad_add_fusion.1.at, ...), custom_call_target="tpu_custom_call" | custom-call | bytes 4194304 | tf_op jit(solution)/shard_map/plane_pick_turned/pallas_call | solution.py:188
  46.4 3.3 %collective-permute-start.8 = (bf16[13,32,128]{2,1,0:T(8,128)(2,1)S(1)}, bf16[13,32,128]{2,1,0:T(8,128)(2,1)S(1)}, u32[]{:S(2)}, u32[]{:S(2)}) collective-permute-start(bf16[13,32,128]{2,1,0:T(8,128)(2,1)S(1)} %get-tuple-element.68), channel_id=1, source_target_pairs={{0,64},{32,96},{64,128},{96,160},{128,192},{160,224},{192,0},{224,... | collective-permute-start | bytes 319496 | tf_op jit(solution)/shard_map/ppermute | solution.py:383
  49.7 4.0 %collective-permute-start.9 = (bf16[13,32,128]{2,1,0:T(8,128)(2,1)S(1)}, bf16[13,32,128]{2,1,0:T(8,128)(2,1)S(1)}, u32[]{:S(2)}, u32[]{:S(2)}) collective-permute-start(bf16[13,32,128]{2,1,0:T(8,128)(2,1)S(1)} %get-tuple-element.69), channel_id=1, source_target_pairs={{0,96},{32,128},{64,160},{96,192},{128,224},{160,0},{192,32},{224,... | collective-permute-start | bytes 319496 | tf_op jit(solution)/shard_map/ppermute | solution.py:383
  54.3 4.9 %collective-permute-start.11 = (bf16[13,32,128]{2,1,0:T(8,128)(2,1)S(1)}, bf16[13,32,128]{2,1,0:T(8,128)(2,1)S(1)}, u32[]{:S(2)}, u32[]{:S(2)}) collective-permute-start(bf16[13,32,128]{2,1,0:T(8,128)(2,1)S(1)} %get-tuple-element.71), channel_id=1, source_target_pairs={{0,160},{32,192},{64,224},{96,0},{128,32},{160,64},{192,96},{224,1... | collective-permute-start | bytes 319496 | tf_op jit(solution)/shard_map/ppermute | solution.py:383
  59.2 2.7 %collective-permute-start.12 = (bf16[13,32,128]{2,1,0:T(8,128)(2,1)S(1)}, bf16[13,32,128]{2,1,0:T(8,128)(2,1)S(1)}, u32[]{:S(2)}, u32[]{:S(2)}) collective-permute-start(bf16[13,32,128]{2,1,0:T(8,128)(2,1)S(1)} %get-tuple-element.72), channel_id=1, source_target_pairs={{0,192},{32,224},{64,0},{96,32},{128,64},{160,96},{192,128},{224,1... | collective-permute-start | bytes 319496 | tf_op jit(solution)/shard_map/ppermute | solution.py:383
  61.9 2.8 %collective-permute-start.13 = (bf16[13,32,128]{2,1,0:T(8,128)(2,1)S(1)}, bf16[13,32,128]{2,1,0:T(8,128)(2,1)S(1)}, u32[]{:S(2)}, u32[]{:S(2)}) collective-permute-start(bf16[13,32,128]{2,1,0:T(8,128)(2,1)S(1)} %get-tuple-element.73), channel_id=1, source_target_pairs={{0,224},{32,0},{64,32},{96,64},{128,96},{160,128},{192,160},{224,1... | collective-permute-start | bytes 319496 | tf_op jit(solution)/shard_map/ppermute | solution.py:383
  64.8 3.5 %collective-permute-done.9.rest_3_ = bf16[13,32,128]{2,1,0:T(8,128)(2,1)S(1)} collective-permute-done((bf16[13,32,128]{2,1,0:T(8,128)(2,1)S(1)}, bf16[13,32,128]{2,1,0:T(8,128)(2,1)S(1)}, u32[]{:S(2)}, u32[]{:S(2)}) %collective-permute-start.9) | collective-permute-done | bytes 106528 | tf_op jit(solution)/shard_map/ppermute | solution.py:383
  68.3 4.0 %collective-permute-done.11.rest_5_ = bf16[13,32,128]{2,1,0:T(8,128)(2,1)S(1)} collective-permute-done((bf16[13,32,128]{2,1,0:T(8,128)(2,1)S(1)}, bf16[13,32,128]{2,1,0:T(8,128)(2,1)S(1)}, u32[]{:S(2)}, u32[]{:S(2)}) %collective-permute-start.11) | collective-permute-done | bytes 106528 | tf_op jit(solution)/shard_map/ppermute | solution.py:383
  76.0 2.9 %plane_pick.1 = bf16[8,13,32,128]{3,2,1,0:T(8,128)(2,1)} custom-call(s32[13]{0:T(128)S(1)} %bitcast.56, bf16[8,8,32,480]{3,2,1,0:T(8,128)(2,1)S(1)} %all-to-all-done.3.got, bf16[20,32,128]{2,1,0:T(8,128)(2,1)S(1)} %get-tuple-element.74.after.rest_0_), custom_call_target="tpu_custom_call" | custom-call | bytes 4194304 | tf_op jit(solution)/shard_map/plane_pick/pallas_call | solution.py:212
  78.8 4.8 %all-to-all-start.4 = ((bf16[8,13,32,128]{3,2,1,0:T(8,128)(2,1)}), bf16[8,13,32,128]{3,2,1,0:T(8,128)(2,1)S(1)}, u32[]{:S(2)}, u32[]{:S(2)}) async-start(bf16[8,13,32,128]{3,2,1,0:T(8,128)(2,1)} %plane_pick.1), calls=%async_computation.4 | async-start | bytes 1703936 | tf_op jit(solution)/shard_map/all_to_all | solution.py:388
  88.3 3.0 %collective-permute-start.15 = (bf16[20,32,128]{2,1,0:T(8,128)(2,1)S(1)}, bf16[20,32,128]{2,1,0:T(8,128)(2,1)S(1)}, u32[]{:S(2)}, u32[]{:S(2)}) collective-permute-start(bf16[20,32,128]{2,1,0:T(8,128)(2,1)S(1)} %get-tuple-element.77), channel_id=1, source_target_pairs={{0,2},{1,3},{2,0},{3,1},{4,6},{5,7},{6,4},{7,5},{8,10},{9,11},{10,... | collective-permute-start | bytes 491528 | tf_op jit(solution)/shard_map/ppermute | solution.py:374
  94.1 2.4 %collective-permute-start.19 = (bf16[20,32,128]{2,1,0:T(8,128)(2,1)S(1)}, bf16[20,32,128]{2,1,0:T(8,128)(2,1)S(1)}, u32[]{:S(2)}, u32[]{:S(2)}) collective-permute-start(bf16[20,32,128]{2,1,0:T(8,128)(2,1)S(1)} %get-tuple-element.81), channel_id=1, source_target_pairs={{0,3},{1,0},{2,1},{3,2},{4,7},{5,4},{6,5},{7,6},{8,11},{9,8},{10,9... | collective-permute-start | bytes 491528 | tf_op jit(solution)/shard_map/ppermute | solution.py:374
  96.6 2.9 %collective-permute-done.15.rest_2_ = bf16[20,32,128]{2,1,0:T(8,128)(2,1)S(1)} collective-permute-done((bf16[20,32,128]{2,1,0:T(8,128)(2,1)S(1)}, bf16[20,32,128]{2,1,0:T(8,128)(2,1)S(1)}, u32[]{:S(2)}, u32[]{:S(2)}) %collective-permute-start.15) | collective-permute-done | bytes 163872 | tf_op jit(solution)/shard_map/ppermute | solution.py:374
  100.4 3.7 %coef_join.1.coef = bf16[80,128,128]{2,1,0:T(8,128)(2,1)S(1)} custom-call(s32[2]{0:T(128)S(1)} %pad_add_fusion.me.after, s32[320]{0:T(512)S(1)} %sub.11.pos, bf16[20,32,128]{2,1,0:T(8,128)(2,1)S(1)} %get-tuple-element.75.rest_0_, bf16[20,32,128]{2,1,0:T(8,128)(2,1)S(1)} %collective-permute-done.14.rest_1_, ...), custom_call_target="tpu_custom_call" | custom-call | bytes 4194304 | tf_op jit(solution)/shard_map/coef_join/pallas_call | solution.py:81
  112.1 3.0 %collective-permute-start.21 = (bf16[20,32,128]{2,1,0:T(8,128)(2,1)S(1)}, bf16[20,32,128]{2,1,0:T(8,128)(2,1)S(1)}, u32[]{:S(2)}, u32[]{:S(2)}) collective-permute-start(bf16[20,32,128]{2,1,0:T(8,128)(2,1)S(1)} %get-tuple-element.84), channel_id=1, source_target_pairs={{0,2},{1,3},{2,0},{3,1},{4,6},{5,7},{6,4},{7,5},{8,10},{9,11},{10,... | collective-permute-start | bytes 491528 | tf_op jit(solution)/shard_map/ppermute | solution.py:374
  118.6 2.8 %collective-permute-done.21.rest_2_ = bf16[20,32,128]{2,1,0:T(8,128)(2,1)S(1)} collective-permute-done((bf16[20,32,128]{2,1,0:T(8,128)(2,1)S(1)}, bf16[20,32,128]{2,1,0:T(8,128)(2,1)S(1)}, u32[]{:S(2)}, u32[]{:S(2)}) %collective-permute-start.21) | collective-permute-done | bytes 163872 | tf_op jit(solution)/shard_map/ppermute | solution.py:374
  121.4 5.5 %product1.3 = bf16[2,1,80,128,128]{4,3,2,1,0:T(8,128)(2,1)} custom-call(s32[2]{0:T(128)S(1)} %pad_add_fusion.me.after, s32[320]{0:T(512)S(1)} %sub.11.pos, bf16[80,128,128]{2,1,0:T(8,128)(2,1)} %copy-done.5, bf16[20,32,128]{2,1,0:T(8,128)(2,1)S(1)} %get-tuple-element.82.rest_0_, ...), custom_call_target="tpu_custom_call", output_to_operand_aliasing={{}: (7, {})} | custom-call | flops 335544320 | bytes 6291456 | tf_op jit(solution)/shard_map/product1/pallas_call | solution.py:281
  (97 shorter events, 35.2 us)
Async XLA Ops:
  3.7 6.4 %collective-permute-start = (bf16[8,32,480]{2,1,0:T(8,128)(2,1)S(1)}, bf16[8,32,480]{2,1,0:T(8,128)(2,1)S(1)}, u32[]{:S(2)}, u32[]{:S(2)}) collective-permute-start(bf16[8,32,480]{2,1,0:T(8,128)(2,1)S(1)} %get-tuple-element.59), channel_id=1, source_target_pairs={{0,4},{4,0},{8,12},{12,8},{16,20},{20,16},{24,28},{28,24},{1,5},{5... | collective-permute-start | bytes 737288 | tf_op jit(solution)/shard_map/ppermute | solution.py:326
  3.7 9.1 %collective-permute-start.1 = (bf16[8,32,480]{2,1,0:T(8,128)(2,1)S(1)}, bf16[8,32,480]{2,1,0:T(8,128)(2,1)S(1)}, u32[]{:S(2)}, u32[]{:S(2)}) collective-permute-start(bf16[8,32,480]{2,1,0:T(8,128)(2,1)S(1)} %get-tuple-element.60), channel_id=1, source_target_pairs={{0,8},{4,12},{8,16},{12,20},{16,24},{20,28},{24,0},{28,4},{1,9},{5... | collective-permute-start | bytes 737288 | tf_op jit(solution)/shard_map/ppermute | solution.py:326
  4.9 12.7 %collective-permute-start.2 = (bf16[8,32,480]{2,1,0:T(8,128)(2,1)S(1)}, bf16[8,32,480]{2,1,0:T(8,128)(2,1)S(1)}, u32[]{:S(2)}, u32[]{:S(2)}) collective-permute-start(bf16[8,32,480]{2,1,0:T(8,128)(2,1)S(1)} %get-tuple-element.61), channel_id=1, source_target_pairs={{0,12},{4,8},{8,20},{12,16},{16,28},{20,24},{24,4},{28,0},{1,13},{... | collective-permute-start | bytes 737288 | tf_op jit(solution)/shard_map/ppermute | solution.py:326
  7.0 17.4 %collective-permute-start.3 = (bf16[8,32,480]{2,1,0:T(8,128)(2,1)S(1)}, bf16[8,32,480]{2,1,0:T(8,128)(2,1)S(1)}, u32[]{:S(2)}, u32[]{:S(2)}) collective-permute-start(bf16[8,32,480]{2,1,0:T(8,128)(2,1)S(1)} %get-tuple-element.62), channel_id=1, source_target_pairs={{0,16},{4,20},{8,24},{12,28},{16,0},{20,4},{24,8},{28,12},{1,17},{... | collective-permute-start | bytes 737288 | tf_op jit(solution)/shard_map/ppermute | solution.py:326
  7.0 22.6 %collective-permute-start.4 = (bf16[8,32,480]{2,1,0:T(8,128)(2,1)S(1)}, bf16[8,32,480]{2,1,0:T(8,128)(2,1)S(1)}, u32[]{:S(2)}, u32[]{:S(2)}) collective-permute-start(bf16[8,32,480]{2,1,0:T(8,128)(2,1)S(1)} %get-tuple-element.63), channel_id=1, source_target_pairs={{0,20},{4,16},{8,28},{12,24},{16,4},{20,0},{24,12},{28,8},{1,21},{... | collective-permute-start | bytes 737288 | tf_op jit(solution)/shard_map/ppermute | solution.py:326
  10.1 31.2 %collective-permute-start.5 = (bf16[8,32,480]{2,1,0:T(8,128)(2,1)}, bf16[8,32,480]{2,1,0:T(8,128)(2,1)}, u32[]{:S(2)}, u32[]{:S(2)}) collective-permute-start(bf16[8,32,480]{2,1,0:T(8,128)(2,1)} %get-tuple-element.64), channel_id=1, source_target_pairs={{0,24},{4,28},{8,0},{12,4},{16,8},{20,12},{24,16},{28,20},{1,25},{... | collective-permute-start | bytes 737288 | tf_op jit(solution)/shard_map/ppermute | solution.py:326
  12.8 28.5 %collective-permute-start.6 = (bf16[8,32,480]{2,1,0:T(8,128)(2,1)}, bf16[8,32,480]{2,1,0:T(8,128)(2,1)}, u32[]{:S(2)}, u32[]{:S(2)}) collective-permute-start(bf16[8,32,480]{2,1,0:T(8,128)(2,1)} %get-tuple-element.65), channel_id=1, source_target_pairs={{0,28},{4,24},{8,4},{12,0},{16,12},{20,8},{24,20},{28,16},{1,29},{... | collective-permute-start | bytes 737288 | tf_op jit(solution)/shard_map/ppermute | solution.py:326
  32.5 43.4 %all-to-all-start.3 = ((bf16[8,8,32,480]{3,2,1,0:T(8,128)(2,1)}), bf16[8,8,32,480]{3,2,1,0:T(8,128)(2,1)S(1)}, u32[]{:S(2)}, u32[]{:S(2)}) async-start(bf16[8,8,32,480]{3,2,1,0:T(8,128)(2,1)} %copy-done), calls=%async_computation.3 | async-start | bytes 4194304 | tf_op jit(solution)/shard_map/all_to_all | solution.py:330
  45.2 14.0 %collective-permute-start.7 = (bf16[13,32,128]{2,1,0:T(8,128)(2,1)S(1)}, bf16[13,32,128]{2,1,0:T(8,128)(2,1)S(1)}, u32[]{:S(2)}, u32[]{:S(2)}) collective-permute-start(bf16[13,32,128]{2,1,0:T(8,128)(2,1)S(1)} %get-tuple-element.67), channel_id=1, source_target_pairs={{0,32},{32,64},{64,96},{96,128},{128,160},{160,192},{192,224},{224... | collective-permute-start | bytes 319496 | tf_op jit(solution)/shard_map/ppermute | solution.py:383
  46.4 15.5 %collective-permute-start.8 = (bf16[13,32,128]{2,1,0:T(8,128)(2,1)S(1)}, bf16[13,32,128]{2,1,0:T(8,128)(2,1)S(1)}, u32[]{:S(2)}, u32[]{:S(2)}) collective-permute-start(bf16[13,32,128]{2,1,0:T(8,128)(2,1)S(1)} %get-tuple-element.68), channel_id=1, source_target_pairs={{0,64},{32,96},{64,128},{96,160},{128,192},{160,224},{192,0},{224,... | collective-permute-start | bytes 319496 | tf_op jit(solution)/shard_map/ppermute | solution.py:383
  49.7 18.6 %collective-permute-start.9 = (bf16[13,32,128]{2,1,0:T(8,128)(2,1)S(1)}, bf16[13,32,128]{2,1,0:T(8,128)(2,1)S(1)}, u32[]{:S(2)}, u32[]{:S(2)}) collective-permute-start(bf16[13,32,128]{2,1,0:T(8,128)(2,1)S(1)} %get-tuple-element.69), channel_id=1, source_target_pairs={{0,96},{32,128},{64,160},{96,192},{128,224},{160,0},{192,32},{224,... | collective-permute-start | bytes 319496 | tf_op jit(solution)/shard_map/ppermute | solution.py:383
  53.7 14.6 %collective-permute-start.10 = (bf16[13,32,128]{2,1,0:T(8,128)(2,1)S(1)}, bf16[13,32,128]{2,1,0:T(8,128)(2,1)S(1)}, u32[]{:S(2)}, u32[]{:S(2)}) collective-permute-start(bf16[13,32,128]{2,1,0:T(8,128)(2,1)S(1)} %get-tuple-element.70), channel_id=1, source_target_pairs={{0,128},{32,160},{64,192},{96,224},{128,0},{160,32},{192,64},{224,... | collective-permute-start | bytes 319496 | tf_op jit(solution)/shard_map/ppermute | solution.py:383
  54.3 18.0 %collective-permute-start.11 = (bf16[13,32,128]{2,1,0:T(8,128)(2,1)S(1)}, bf16[13,32,128]{2,1,0:T(8,128)(2,1)S(1)}, u32[]{:S(2)}, u32[]{:S(2)}) collective-permute-start(bf16[13,32,128]{2,1,0:T(8,128)(2,1)S(1)} %get-tuple-element.71), channel_id=1, source_target_pairs={{0,160},{32,192},{64,224},{96,0},{128,32},{160,64},{192,96},{224,1... | collective-permute-start | bytes 319496 | tf_op jit(solution)/shard_map/ppermute | solution.py:383
  59.2 15.2 %collective-permute-start.12 = (bf16[13,32,128]{2,1,0:T(8,128)(2,1)S(1)}, bf16[13,32,128]{2,1,0:T(8,128)(2,1)S(1)}, u32[]{:S(2)}, u32[]{:S(2)}) collective-permute-start(bf16[13,32,128]{2,1,0:T(8,128)(2,1)S(1)} %get-tuple-element.72), channel_id=1, source_target_pairs={{0,192},{32,224},{64,0},{96,32},{128,64},{160,96},{192,128},{224,1... | collective-permute-start | bytes 319496 | tf_op jit(solution)/shard_map/ppermute | solution.py:383
  61.9 13.2 %collective-permute-start.13 = (bf16[13,32,128]{2,1,0:T(8,128)(2,1)S(1)}, bf16[13,32,128]{2,1,0:T(8,128)(2,1)S(1)}, u32[]{:S(2)}, u32[]{:S(2)}) collective-permute-start(bf16[13,32,128]{2,1,0:T(8,128)(2,1)S(1)} %get-tuple-element.73), channel_id=1, source_target_pairs={{0,224},{32,0},{64,32},{96,64},{128,96},{160,128},{192,160},{224,1... | collective-permute-start | bytes 319496 | tf_op jit(solution)/shard_map/ppermute | solution.py:383
  78.8 30.8 %all-to-all-start.4 = ((bf16[8,13,32,128]{3,2,1,0:T(8,128)(2,1)}), bf16[8,13,32,128]{3,2,1,0:T(8,128)(2,1)S(1)}, u32[]{:S(2)}, u32[]{:S(2)}) async-start(bf16[8,13,32,128]{3,2,1,0:T(8,128)(2,1)} %plane_pick.1), calls=%async_computation.4 | async-start | bytes 1703936 | tf_op jit(solution)/shard_map/all_to_all | solution.py:388
  86.3 7.8 %collective-permute-start.14 = (bf16[20,32,128]{2,1,0:T(8,128)(2,1)S(1)}, bf16[20,32,128]{2,1,0:T(8,128)(2,1)S(1)}, u32[]{:S(2)}, u32[]{:S(2)}) collective-permute-start(bf16[20,32,128]{2,1,0:T(8,128)(2,1)S(1)} %get-tuple-element.76), channel_id=1, source_target_pairs={{0,1},{1,2},{2,3},{3,0},{4,5},{5,6},{6,7},{7,4},{8,9},{9,10},{10,1... | collective-permute-start | bytes 491528 | tf_op jit(solution)/shard_map/ppermute | solution.py:374
  88.3 11.2 %collective-permute-start.15 = (bf16[20,32,128]{2,1,0:T(8,128)(2,1)S(1)}, bf16[20,32,128]{2,1,0:T(8,128)(2,1)S(1)}, u32[]{:S(2)}, u32[]{:S(2)}) collective-permute-start(bf16[20,32,128]{2,1,0:T(8,128)(2,1)S(1)} %get-tuple-element.77), channel_id=1, source_target_pairs={{0,2},{1,3},{2,0},{3,1},{4,6},{5,7},{6,4},{7,5},{8,10},{9,11},{10,... | collective-permute-start | bytes 491528 | tf_op jit(solution)/shard_map/ppermute | solution.py:374
  91.3 9.1 %collective-permute-start.16 = (bf16[20,32,128]{2,1,0:T(8,128)(2,1)S(1)}, bf16[20,32,128]{2,1,0:T(8,128)(2,1)S(1)}, u32[]{:S(2)}, u32[]{:S(2)}) collective-permute-start(bf16[20,32,128]{2,1,0:T(8,128)(2,1)S(1)} %get-tuple-element.78), channel_id=1, source_target_pairs={{0,3},{1,0},{2,1},{3,2},{4,7},{5,4},{6,5},{7,6},{8,11},{9,8},{10,9... | collective-permute-start | bytes 491528 | tf_op jit(solution)/shard_map/ppermute | solution.py:374
  92.6 11.5 %collective-permute-start.17 = (bf16[20,32,128]{2,1,0:T(8,128)(2,1)S(1)}, bf16[20,32,128]{2,1,0:T(8,128)(2,1)S(1)}, u32[]{:S(2)}, u32[]{:S(2)}) collective-permute-start(bf16[20,32,128]{2,1,0:T(8,128)(2,1)S(1)} %get-tuple-element.79), channel_id=1, source_target_pairs={{0,1},{1,2},{2,3},{3,0},{4,5},{5,6},{6,7},{7,4},{8,9},{9,10},{10,1... | collective-permute-start | bytes 491528 | tf_op jit(solution)/shard_map/ppermute | solution.py:374
  93.3 11.9 %collective-permute-start.18 = (bf16[20,32,128]{2,1,0:T(8,128)(2,1)S(1)}, bf16[20,32,128]{2,1,0:T(8,128)(2,1)S(1)}, u32[]{:S(2)}, u32[]{:S(2)}) collective-permute-start(bf16[20,32,128]{2,1,0:T(8,128)(2,1)S(1)} %get-tuple-element.80), channel_id=1, source_target_pairs={{0,2},{1,3},{2,0},{3,1},{4,6},{5,7},{6,4},{7,5},{8,10},{9,11},{10,... | collective-permute-start | bytes 491528 | tf_op jit(solution)/shard_map/ppermute | solution.py:374
  94.1 11.1 %collective-permute-start.19 = (bf16[20,32,128]{2,1,0:T(8,128)(2,1)S(1)}, bf16[20,32,128]{2,1,0:T(8,128)(2,1)S(1)}, u32[]{:S(2)}, u32[]{:S(2)}) collective-permute-start(bf16[20,32,128]{2,1,0:T(8,128)(2,1)S(1)} %get-tuple-element.81), channel_id=1, source_target_pairs={{0,3},{1,0},{2,1},{3,2},{4,7},{5,4},{6,5},{7,6},{8,11},{9,8},{10,9... | collective-permute-start | bytes 491528 | tf_op jit(solution)/shard_map/ppermute | solution.py:374
  110.5 8.2 %collective-permute-start.20 = (bf16[20,32,128]{2,1,0:T(8,128)(2,1)S(1)}, bf16[20,32,128]{2,1,0:T(8,128)(2,1)S(1)}, u32[]{:S(2)}, u32[]{:S(2)}) collective-permute-start(bf16[20,32,128]{2,1,0:T(8,128)(2,1)S(1)} %get-tuple-element.83), channel_id=1, source_target_pairs={{0,1},{1,2},{2,3},{3,0},{4,5},{5,6},{6,7},{7,4},{8,9},{9,10},{10,1... | collective-permute-start | bytes 491528 | tf_op jit(solution)/shard_map/ppermute | solution.py:374
  112.1 9.3 %collective-permute-start.21 = (bf16[20,32,128]{2,1,0:T(8,128)(2,1)S(1)}, bf16[20,32,128]{2,1,0:T(8,128)(2,1)S(1)}, u32[]{:S(2)}, u32[]{:S(2)}) collective-permute-start(bf16[20,32,128]{2,1,0:T(8,128)(2,1)S(1)} %get-tuple-element.84), channel_id=1, source_target_pairs={{0,2},{1,3},{2,0},{3,1},{4,6},{5,7},{6,4},{7,5},{8,10},{9,11},{10,... | collective-permute-start | bytes 491528 | tf_op jit(solution)/shard_map/ppermute | solution.py:374
  (11 other events, 41.6 us)

commit v2 on v0

--- a/solution.py
+++ b/solution.py
@@ -9,7 +9,7 @@
 
 BLK = 128
 NZ, NX, NCORE = 8, 4, 2
-LEVELS = (13, 30)
+LEVELS = (5, 6, 8)
 BF = jnp.bfloat16
 VMEM = pl.BlockSpec(memory_space=pltpu.VMEM)
 ANY = pl.BlockSpec(memory_space=pl.ANY)
@@ -89,96 +89,110 @@
     )(me, pos, *pieces)
 
 
-def plane_split_kernel(batch, at, pairs, *rest):
+def core_split_kernel(at, pairs, *rest):
     outs, sems = rest[:-1], rest[-1]
     copies = []
     for k, out in enumerate(outs):
-        px = turn(at[0], k // NCORE, NX)
-        pc = at[1] if k % NCORE == 0 else 1 - at[1]
-        copies.append(pltpu.make_async_copy(pairs.at[batch, :, px, pc], out, sems.at[k]))
+        core = at[1] if k % 2 == 0 else 1 - at[1]
+        copies.append(pltpu.make_async_copy(pairs.at[k // 2, :, :, core], out, sems.at[k]))
     for copy in copies:
         copy.start()
     for copy in copies:
         copy.wait()
 
 
-def plane_split(batch, at, pairs):
-    _, nz, nx, nc, occ, width = pairs.shape
-    return pl.pallas_call(
-        functools.partial(plane_split_kernel, batch),
-        out_shape=[jax.ShapeDtypeStruct((nz, occ, width), BF)] * (nx * nc),
+def core_split(at, pairs):
+    nb, nz, nx, _, occ, width = pairs.shape
+    return pl.pallas_call(
+        core_split_kernel,
+        out_shape=[jax.ShapeDtypeStruct((nz, nx, occ, width), BF)] * (2 * nb),
         in_specs=[SMEM, pl.BlockSpec(memory_space=pltpu.HBM)],
-        out_specs=[VMEM] * (nx * nc),
-        scratch_shapes=[pltpu.SemaphoreType.DMA((nx * nc,))],
-        compiler_params=params(60),
+        out_specs=[VMEM] * (2 * nb),
+        scratch_shapes=[pltpu.SemaphoreType.DMA((2 * nb,))],
+        compiler_params=params(12),
+        cost_estimate=cost(8 << 20),
+        name="core_split",
+    )(at, pairs)
+
+
+def cut_tiles(odd, left, right, tiles):
+    nz, nx, occ, width = left.shape
+
+    def row(i, _):
+        z, x = i // nx, i % nx
+
+        def span(lo, hi):
+            parts = []
+            if lo < width:
+                parts.append(left[z, x, :, lo : min(hi, width)])
+            if hi > width:
+                parts.append(right[z, x, :, max(lo, width) - width : hi - width])
+            return parts
+
+        half = [jnp.zeros((occ, BLK // 2), BF)]
+        for t in range(tiles.shape[1]):
+            lo = t * BLK - (BLK // 2 if odd else 0)
+            hi = lo + BLK
+            parts = span(max(lo, 0), min(hi, 2 * width))
+            if lo < 0:
+                parts = half + parts
+            if hi > 2 * width:
+                parts = parts + half
+            tiles[i, t] = parts[0] if len(parts) == 1 else jnp.concatenate(parts, axis=1)
+        return 0
+
+    lax.fori_loop(0, nz * nx, row, 0)
+
+
+def tile_pick_kernel(at, listed, own, got, after, out, tiles):
+    for odd in (0, 1):
+        for core in (0, 1):
+            left, right = (own, got) if core == 0 else (got, own)
+
+            @pl.when((at[0] % 2 == odd) & (at[1] == core))
+            def _():
+                cut_tiles(odd, left, right, tiles)
+
+    def keep(i, _):
+        for j in range(out.shape[1]):
+            out[i, j] = tiles[i, listed[j]]
+        return 0
+
+    lax.fori_loop(0, out.shape[0], keep, 0, unroll=2)
+
+
+def tile_pick(at, listed, own, got, after, cap):
+    nz, nx, occ, width = own.shape
+    held = -(-2 * width // BLK)
+    return pl.pallas_call(
+        tile_pick_kernel,
+        out_shape=jax.ShapeDtypeStruct((nz * nx, cap, occ, BLK), BF),
+        in_specs=[SMEM, SMEM, VMEM, VMEM, ANY],
+        out_specs=VMEM,
+        scratch_shapes=[pltpu.VMEM((nz * nx, held, occ, BLK), BF)],
+        compiler_params=params(16),
         cost_estimate=cost(4 << 20),
-        name=f"plane_split{batch}",
-    )(at, pairs)
-
-
-def plane_pick_kernel(at, listed, *rest):
-    pieces, (out, got, tiles) = rest[:-3], rest[-3:]
-    width = got.shape[3]
-    blocks = tiles.shape[1]
-    for k, piece in enumerate(pieces):
-        sx = turn(at[0], -(k // NCORE), NX)
-        sc = at[1] if k % NCORE == 0 else 1 - at[1]
-        got[sx * NCORE + sc] = piece[...]
-
-    def cut(pz, _):
-        for j in range(blocks):
-            src, off = divmod(j * BLK, width)
-            if off + BLK <= width:
-                tiles[pz, j] = got[src, pz, :, off : off + BLK]
-            else:
-                tiles[pz, j] = jnp.concatenate(
-                    [got[src, pz, :, off:width], got[src + 1, pz, :, : off + BLK - width]], axis=1
-                )
-        return 0
-
-    lax.fori_loop(0, NZ, cut, 0)
-
-    def keep(j, _):
-        block = listed[j]
-        for pz in range(NZ):
-            out[pz, j] = tiles[pz, block]
-        return 0
-
-    lax.fori_loop(0, out.shape[1], keep, 0)
-
-
-def plane_pick(at, listed, pieces, cap):
-    nz, occ, width = pieces[0].shape
-    n = len(pieces)
-    return pl.pallas_call(
-        plane_pick_kernel,
-        out_shape=jax.ShapeDtypeStruct((nz, cap, occ, BLK), BF),
-        in_specs=[SMEM, SMEM] + [VMEM] * n,
-        out_specs=VMEM,
-        scratch_shapes=[
-            pltpu.VMEM((n, nz, occ, width), BF),
-            pltpu.VMEM((nz, n * width // BLK, occ, BLK), BF),
-        ],
-        compiler_params=params(24),
-        cost_estimate=cost(4 << 20),
-        name="plane_pick",
-    )(at, listed, *pieces)
-
-
-def slot_pick_kernel(me, plane, rank, got, *outs):
-    slots = outs[0].shape[0]
+        name="tile_pick",
+    )(at, listed, own, got, after)
+
+
+def slot_pick_kernel(me, first, second, got, *outs):
+    cap = got.shape[1]
+    slots, occ, _ = outs[0].shape
+    low = lax.broadcasted_iota(jnp.int32, (occ, BLK), 1) < BLK // 2
     for k, out in enumerate(outs):
         base = turn(me[0], k, len(outs)) * slots
 
         def step(t, _):
-            out[t] = got[plane[base + t], rank[base + t]]
+            a, b = first[base + t], second[base + t]
+            out[t] = jnp.where(low, got[a // cap, a % cap], got[b // cap, b % cap])
             return 0
 
         lax.fori_loop(0, slots, step, 0, unroll=4)
 
 
-def slot_pick(me, plane, rank, got, groups):
-    slots = plane.shape[0] // groups
+def slot_pick(me, first, second, got, groups):
+    slots = first.shape[0] // groups
     occ = got.shape[2]
     return pl.pallas_call(
         slot_pick_kernel,
@@ -188,7 +202,7 @@
         compiler_params=params(16),
         cost_estimate=cost(2 << 20),
         name="slot_pick",
-    )(me, plane, rank, got)
+    )(me, first, second, got)
 
 
 def product_kernel(per, groups, me, pos, coef, *rest):
@@ -237,8 +251,6 @@
     groups = lax.axis_size("sp")
     basis = occ_coef.shape[0]
     nblk = basis // BLK
-    per_plane = nblk // NZ
-    plane_devs = NX * NCORE
     total_blocks = block_coords.shape[0]
     owned = total_blocks // groups
     capacity = block_lists.shape[2]
@@ -248,20 +260,13 @@
     at = jnp.stack([lax.axis_index("x"), lax.axis_index("core")]).astype(jnp.int32)
     pairs = gamma_pairs.reshape(batches, NZ, NX, NCORE, occ, width)
 
-    def exchange_plane(split):
-        got = [split[0]]
-        for k in range(1, plane_devs):
-            dx, dc = divmod(k, NCORE)
-            moves = [
-                (x * NCORE + c, (x + dx) % NX * NCORE + (c ^ dc))
-                for x in range(NX)
-                for c in range(NCORE)
-            ]
-            got.append(lax.ppermute(split[k], ("x", "core"), moves))
-        return got
-
-    got0 = exchange_plane(plane_split(0, at, pairs))
-    split1 = plane_split(1, at, pairs)
+    pairs = pltpu.with_memory_space_constraint(pairs, pltpu.HBM)
+
+    halves = core_split(at, pairs)
+    halves0, halves1 = (
+        (halves[2 * b], lax.ppermute(halves[2 * b + 1], "core", [(0, 1), (1, 0)]))
+        for b in range(batches)
+    )
 
     valid = jnp.arange(capacity, dtype=jnp.int32)[None, None, :] < block_counts[:, :, None]
     lists = jnp.clip(block_lists, 0, owned - 1)
@@ -271,25 +276,38 @@
     col_ids = jnp.sum(jnp.where(hit, block_coords[:, 1], 0), axis=2)
     live_col = jnp.where(valid.reshape(groups, -1), col_ids, -1)
     need = jnp.any(live_col[:, :, None] == jnp.arange(nblk, dtype=jnp.int32), axis=1)
-    need = need.reshape(groups, NZ, per_plane).astype(jnp.int32)
+    pair_blocks = 2 * nblk // (NZ * NX)
+    held = -(-2 * width // BLK)
+    need = need.reshape(groups, NZ * NX // 2, 1, pair_blocks).astype(jnp.int32)
+    need = jnp.concatenate([need[..., :held], need[..., pair_blocks - held :]], axis=2)
+    need = need.reshape(groups, NZ * NX, held)
     most = jnp.max(jnp.sum(need, axis=2))
     my_need = lax.dynamic_index_in_dim(need, me_s, 0, keepdims=False)
-    plane_ids = jnp.arange(per_plane, dtype=jnp.int32)
-    before = (plane_ids[None, :] < plane_ids[:, None]).astype(jnp.int32)
+    tile_ids = jnp.arange(held, dtype=jnp.int32)
+    before = (tile_ids[None, :] < tile_ids[:, None]).astype(jnp.int32)
     rank = jnp.sum(my_need[:, None, :] * before[None], axis=2)
     my_cols = lax.dynamic_index_in_dim(col_ids, me_s, 0, keepdims=False)
     my_rows = lax.dynamic_index_in_dim(row_ids, me_s, 0, keepdims=False)
     my_live = lax.dynamic_index_in_dim(valid.reshape(groups, -1), me_s, 0, keepdims=False)
-    col_hit = my_cols[:, None] == jnp.arange(nblk, dtype=jnp.int32)
-    slot_rank = jnp.sum(jnp.where(col_hit, rank.reshape(-1), 0), axis=1)
-    slot_rank = jnp.where(my_live, slot_rank, 0)
-    slot_plane = jnp.where(my_live, my_cols // per_plane, 0)
-    plane_need = lax.dynamic_index_in_dim(my_need, me_z, 0, keepdims=False)
-    plane_rank = lax.dynamic_index_in_dim(rank, me_z, 0, keepdims=False)
+    two_chips, within = my_cols // pair_blocks, my_cols % pair_blocks
+
+    def place(upper):
+        on_odd = within > held - 1 - upper
+        chip = 2 * two_chips + on_odd
+        tile = within - jnp.where(on_odd, pair_blocks - held, 0)
+        hit = (chip * held + tile)[:, None] == jnp.arange(NZ * NX * held, dtype=jnp.int32)
+        order = jnp.sum(jnp.where(hit, rank.reshape(-1), 0), axis=1)
+        return jnp.where(my_live, chip, 0), jnp.where(my_live, order, 0)
+
+    chip_a, rank_a = place(0)
+    chip_b, rank_b = place(1)
+    my_chip = me_z * NX + lax.axis_index("x")
+    chip_need = lax.dynamic_index_in_dim(my_need, my_chip, 0, keepdims=False)
+    chip_rank = lax.dynamic_index_in_dim(rank, my_chip, 0, keepdims=False)
     listed = jnp.sum(
         jnp.where(
-            (plane_rank[None, :] == plane_ids[:, None]) & (plane_need[None, :] > 0),
-            plane_ids[None, :],
+            (chip_rank[None, :] == tile_ids[:, None]) & (chip_need[None, :] > 0),
+            tile_ids[None, :],
             0,
         ),
         axis=1,
@@ -309,37 +327,28 @@
             for k in range(1, groups)
         ]
 
-    def finish(cap, got0, split1, coef_t, my_rows, pos, listed, slot_plane, slot_rank):
-        def planes(got):
-            return lax.all_to_all(plane_pick(at, listed, got, cap), "z", 0, 0, tiled=True)
+    def finish(cap, halves0, halves1, coef_t, my_rows, pos, listed, chip_a, rank_a, chip_b, rank_b):
+        first, second = chip_a * cap + rank_a, chip_b * cap + rank_b
+
+        def tiles(halves, after):
+            picked = tile_pick(at, listed, *halves, after, cap)
+            return picked, lax.all_to_all(picked, ("z", "x"), 0, 0, tiled=True)
 
         def owners(got):
-            return exchange_owners(slot_pick(me, slot_plane, slot_rank, got, groups))
-
-        held0 = planes(got0)
-        got1 = exchange_plane(split1)
-        coef_parts = exchange_owners(coef_pick(me, coef_t, my_rows, got1[1], groups))
+            return exchange_owners(slot_pick(me, first, second, got, groups))
+
+        picked0, got0 = tiles(halves0, me)
+        coef_parts = exchange_owners(coef_pick(me, coef_t, my_rows, picked0, groups))
         coef = coef_join(me, coef_parts, pos, owned)
-        held1 = planes(got1)
-        out = product(0, batches, me, coef, owners(held0), pos, None)
-        return product(1, batches, me, coef, owners(held1), pos, out)
+        _, got1 = tiles(halves1, coef)
+        out = product(0, batches, me, coef, owners(got0), pos, None)
+        return product(1, batches, me, coef, owners(got1), pos, out)
 
     level = jnp.sum((most > jnp.array(LEVELS[:-1], jnp.int32)).astype(jnp.int32))
-    level, my_rows, pos, listed, slot_plane, slot_rank = lax.optimization_barrier(
-        (level, my_rows, pos, listed, slot_plane, slot_rank)
-    )
-    return lax.switch(
-        level,
-        [functools.partial(finish, cap) for cap in LEVELS],
-        got0,
-        split1,
-        occ_coef.T,
-        my_rows,
-        pos,
-        listed,
-        slot_plane,
-        slot_rank,
-    )
+    level, listed = lax.optimization_barrier((level, listed))
+    tables = (my_rows, pos, listed, chip_a, rank_a, chip_b, rank_b)
+    branches = [functools.partial(finish, cap) for cap in LEVELS]
+    return lax.switch(level, branches, halves0, halves1, occ_coef.T, *tables)
 
 
 def solution(mesh):

time: 126 us -> 122 us (0.968)
  starting transfers between devices: 45.7 us -> 35.7 us
  waiting for transfers between devices: 47.7 us -> 39.8 us
  Pallas kernels: 26.4 us -> 32 us
  other arithmetic: 2.56 us -> 7.21 us
  local copies, waits for them, and re-layouts: 1.19 us -> 5.48 us
    ppermute x14 -> x2, waiting for transfers between devices: 34.8 us -> 0.07 us  [local(): lax.ppermute(halves[2 * b + 1], 'core', [(0, 1), (1, 0)])]
    all_to_all x2, waiting for transfers between devices: 12.8 us -> 33.9 us  [tiles(): return (picked, lax.all_to_all(picked, ('z', 'x'), 0, 0, tiled=True))]
    ppermute x14 -> x2, starting transfers between devices: 14.7 us -> 0.59 us  [local(): lax.ppermute(halves[2 * b + 1], 'core', [(0, 1), (1, 0)])]
    ppermute x9, waiting for transfers between devices: 0.02 us -> 5.83 us  [exchange_owners(): lax.ppermute(sent[k], 'sp', [(i, (i + k) % groups) for i in range(groups)])]
    pallas_call x2, Pallas kernels: 1.68 us -> 6.04 us  [slot_pick(): pl.pallas_call(slot_pick_kernel, out_shape=[jax.ShapeDtypeStruct((slots,...]
    reduce_sum x3 -> x4, other arithmetic: 0.43 us -> 2.55 us  [the longest x1 2 us: local(): jnp.sum((most > jnp.array(LEVELS[:-1], jnp.int32)).astype(jnp.int32))]
    ppermute x9, starting transfers between devices: 15.5 us -> 17.6 us  [exchange_owners(): lax.ppermute(sent[k], 'sp', [(i, (i + k) % groups) for i in range(groups)])]
    all_to_all x2, starting transfers between devices: 15.5 us -> 17.5 us  [tiles(): return (picked, lax.all_to_all(picked, ('z', 'x'), 0, 0, tiled=True))]
  transfers between devices with their start and end apart: 25 -> 13, of which waited for: 9 -> 7; matrix products, arithmetic and copies ran while one was open for 3% -> 3% of each run, Pallas kernels for 13% -> 16%
where the time goes in v2:
time: 122 us; the launch traced here: 121 us
  waiting for transfers between devices  39.8 us (33%)
  starting transfers between devices  35.7 us (29%)
  Pallas kernels  32 us (26%)
  other arithmetic  7.21 us (6%)
  local copies, waits for them, and re-layouts  5.48 us (4%)
    all_to_all x2, waiting for transfers between devices, tiles(): return (picked, lax.all_to_all(picked, ('z', 'x'), 0, 0, tiled=True))  33.9 us
    ppermute x9, starting transfers between devices, exchange_owners(): lax.ppermute(sent[k], 'sp', [(i, (i + k) % groups) for i in range(groups)])  17.6 us
    all_to_all x2, starting transfers between devices, tiles(): return (picked, lax.all_to_all(picked, ('z', 'x'), 0, 0, tiled=True))  17.5 us
    pallas_call x2, Pallas kernels, tile_pick(): pl.pallas_call(tile_pick_kernel, out_shape=jax.ShapeDtypeStruct((nz * nx,...  9.98 us
    pallas_call x2, Pallas kernels, product(): pl.pallas_call(functools.partial(product_kernel, per, groups), out_shape=...  6.67 us
    pallas_call x2, Pallas kernels, slot_pick(): pl.pallas_call(slot_pick_kernel, out_shape=[jax.ShapeDtypeStruct((slots,...  6.04 us
    ppermute x9, waiting for transfers between devices, exchange_owners(): lax.ppermute(sent[k], 'sp', [(i, (i + k) % groups) for i in range(groups)])  5.83 us
    pallas_call x1, Pallas kernels, coef_join(): pl.pallas_call(coef_join_kernel, out_shape=jax.ShapeDtypeStruct((owned, B...  3.75 us
  transfers between devices with their start and end apart: 13, of which 7 were waited for; matrix products, arithmetic and copies ran while one was open for 3% of the time, Pallas kernels for 16%

profile of v2, /device:TPU:4, one launch (start us, length us, event | category | flops | bytes accessed | tf_op | source)
XLA Modules:
  0.0 121.1 jit_solution(522685688452369322)
XLA Ops:
  3.9 2.0 %fusion.16 = (s32[]{:T(128)}, s32[2]{0:T(128)S(1)}) fusion(s32[2]{0:T(128)} %constant.118.clone, s32[]{:T(128)} %reduce_max.9, s32[1]{0:T(128)} %bitcast.16, s32[1]{0:T(128)} %bitcast.15), kind=kLoop, calls=%fused_computation.89 | loop fusion | flops 7 | bytes 32 | tf_op jit(solution)/shard_map/reduce_sum | solution.py:347
  5.9 3.7 %core_split.1 = (bf16[8,4,32,480]{3,2,1,0:T(8,128)(2,1)S(1)}, bf16[8,4,32,480]{3,2,1,0:T(8,128)(2,1)S(1)}, bf16[8,4,32,480]{3,2,1,0:T(8,128)(2,1)}, bf16[8,4,32,480]{3,2,1,0:T(8,128)(2,1)S(1)}) custom-call(s32[2]{0:T(128)S(1)} %get-tuple-element.1508.at, bf16[2,8,4,2,32,480]{5,4,3,2,1,0:T(8,128)(2,1)} %bitcast.53), custom_call_target="tpu_custom_call" | custom-call | bytes 8388608 | tf_op jit(solution)/shard_map/core_split/pallas_call | solution.py:106
  15.7 105.5 %conditional.1 = (bf16[2,1,80,128,128]{4,3,2,1,0:T(8,128)(2,1)}) conditional(s32[]{:T(128)} %clamp.10, (s32[2]{0:T(128)S(1)}, s32[8]{0:T(128)S(1)}, bf16[8,4,32,480]{3,2,1,0:T(8,128)(2,1)S(1)}, bf16[8,4,32,480]{3,2,1,0:T(8,128)(2,1)}, s32[]{:T(128)}, /*index=5*/pred[4,80,320]{2,1,0:T(8,128)(4,1)S(1)}, ...), branch_computations={%region_11.12_spmd, %region_12.13_spmd, %region_13.14_spmd} | conditional | flops 671442816 | bytes 61428608 | solution.py:351
  15.7 5.4 %tile_pick.6.after = bf16[32,5,32,128]{3,2,1,0:T(8,128)(2,1)} custom-call(s32[2]{0:T(128)S(1)} %get-tuple-element.97.at, s32[8]{0:T(128)S(1)} %get-tuple-element.98.listed, bf16[8,4,32,480]{3,2,1,0:T(8,128)(2,1)S(1)} %get-tuple-element.99.own, bf16[8,4,32,480]{3,2,1,0:T(8,128)(2,1)} %get-tuple-element.100.got, s32[1]{0:T(128)} %bitcast.after.me), custom_call_target="tpu_custom_call" | custom-call | bytes 4194304 | tf_op jit(solution)/shard_map/cond/branch_0_fun/tile_pick/pallas_call | solution.py:167
  21.1 11.9 %all-to-all-start.1 = ((bf16[32,5,32,128]{3,2,1,0:T(8,128)(2,1)}), bf16[32,5,32,128]{3,2,1,0:T(8,128)(2,1)}, u32[]{:S(2)}, u32[]{:S(2)}) async-start(bf16[32,5,32,128]{3,2,1,0:T(8,128)(2,1)} %tile_pick.6.after), calls=%async_computation.1 | async-start | bytes 2621440 | tf_op jit(solution)/shard_map/cond/branch_0_fun/all_to_all | solution.py:335
  33.1 1.9 %coef_pick.3 = (bf16[20,32,128]{2,1,0:T(8,128)(2,1)S(1)}, bf16[20,32,128]{2,1,0:T(8,128)(2,1)S(1)}, bf16[20,32,128]{2,1,0:T(8,128)(2,1)S(1)}, bf16[20,32,128]{2,1,0:T(8,128)(2,1)S(1)}) custom-call(s32[1]{0:T(128)} %bitcast.after.me, s32[80]{0:T(128)S(1)} %fusion.1.rows, bf16[32,30720]{1,0:T(8,128)(2,1)} %get-tuple-element.96.coef, ...), custom_call_target="tpu_custom_call" | custom-call | bytes 4194304 | tf_op jit(solution)/shard_map/cond/branch_0_fun/coef_pick/pallas_call | solution.py:48
  35.0 1.7 %collective-permute-start = (bf16[20,32,128]{2,1,0:T(8,128)(2,1)S(1)}, bf16[20,32,128]{2,1,0:T(8,128)(2,1)S(1)}, u32[]{:S(2)}, u32[]{:S(2)}) collective-permute-start(bf16[20,32,128]{2,1,0:T(8,128)(2,1)S(1)} %get-tuple-element.102), channel_id=1, source_target_pairs={{0,1},{1,2},{2,3},{3,0},{4,5},{5,6},{6,7},{7,4},{8,9},{9,10},{10,1... | collective-permute-start | bytes 491528 | tf_op jit(solution)/shard_map/cond/branch_0_fun/ppermute | solution.py:326
  36.7 2.9 %collective-permute-start.1 = (bf16[20,32,128]{2,1,0:T(8,128)(2,1)S(1)}, bf16[20,32,128]{2,1,0:T(8,128)(2,1)S(1)}, u32[]{:S(2)}, u32[]{:S(2)}) collective-permute-start(bf16[20,32,128]{2,1,0:T(8,128)(2,1)S(1)} %get-tuple-element.103), channel_id=1, source_target_pairs={{0,2},{1,3},{2,0},{3,1},{4,6},{5,7},{6,4},{7,5},{8,10},{9,11},{10,... | collective-permute-start | bytes 491528 | tf_op jit(solution)/shard_map/cond/branch_0_fun/ppermute | solution.py:326
  39.6 1.3 %collective-permute-start.2 = (bf16[20,32,128]{2,1,0:T(8,128)(2,1)S(1)}, bf16[20,32,128]{2,1,0:T(8,128)(2,1)S(1)}, u32[]{:S(2)}, u32[]{:S(2)}) collective-permute-start(bf16[20,32,128]{2,1,0:T(8,128)(2,1)S(1)} %get-tuple-element.104), channel_id=1, source_target_pairs={{0,3},{1,0},{2,1},{3,2},{4,7},{5,4},{6,5},{7,6},{8,11},{9,8},{10,9... | collective-permute-start | bytes 491528 | tf_op jit(solution)/shard_map/cond/branch_0_fun/ppermute | solution.py:326
  42.3 4.4 %collective-permute-done.1.rest_2_ = bf16[20,32,128]{2,1,0:T(8,128)(2,1)S(1)} collective-permute-done((bf16[20,32,128]{2,1,0:T(8,128)(2,1)S(1)}, bf16[20,32,128]{2,1,0:T(8,128)(2,1)S(1)}, u32[]{:S(2)}, u32[]{:S(2)}) %collective-permute-start.1) | collective-permute-done | bytes 163872 | tf_op jit(solution)/shard_map/cond/branch_0_fun/ppermute | solution.py:326
  46.8 3.7 %coef_join.3.after.coef = bf16[80,128,128]{2,1,0:T(8,128)(2,1)S(1)} custom-call(s32[1]{0:T(128)} %bitcast.after.me, s32[320]{0:T(512)S(1)} %sub.31.pos, bf16[20,32,128]{2,1,0:T(8,128)(2,1)S(1)} %get-tuple-element.101.rest_0_, bf16[20,32,128]{2,1,0:T(8,128)(2,1)S(1)} %collective-permute-done.rest_1_, bf16[20,32,128]{2,1,0:T(8,128)(2,1)S(1)} %collective-permute-done.1.rest_2_, ...), custom_call_target="tpu_custom_call" | custom-call | bytes 4194304 | tf_op jit(solution)/shard_map/cond/branch_0_fun/coef_join/pallas_call | solution.py:80
  50.5 4.6 %tile_pick.7 = bf16[32,5,32,128]{3,2,1,0:T(8,128)(2,1)S(1)} custom-call(s32[2]{0:T(128)S(1)} %get-tuple-element.97.at, s32[8]{0:T(128)} %copy-done.18, bf16[8,4,32,480]{3,2,1,0:T(8,128)(2,1)} %get-tuple-element.109.own, bf16[8,4,32,480]{3,2,1,0:T(8,128)(2,1)} %get-tuple-element.110.got, bf16[80,128,128]{2,1,0:T(8,128)(2,1)S(1)} %coef_join.3.after.coef), custom_call_target="tpu_custom_call" | custom-call | bytes 4194304 | tf_op jit(solution)/shard_map/cond/branch_0_fun/tile_pick/pallas_call | solution.py:167
  56.2 10.7 %all-to-all-done.1.got = bf16[32,5,32,128]{3,2,1,0:T(8,128)(2,1)} async-done(((bf16[32,5,32,128]{3,2,1,0:T(8,128)(2,1)}), bf16[32,5,32,128]{3,2,1,0:T(8,128)(2,1)}, u32[]{:S(2)}, u32[]{:S(2)}) %all-to-all-start.1) | async-done | bytes 1310752 | tf_op jit(solution)/shard_map/cond/branch_0_fun/all_to_all | solution.py:335
  67.0 5.6 %all-to-all-start = ((bf16[32,5,32,128]{3,2,1,0:T(8,128)(2,1)}), bf16[32,5,32,128]{3,2,1,0:T(8,128)(2,1)}, u32[]{:S(2)}, u32[]{:S(2)}) async-start(bf16[32,5,32,128]{3,2,1,0:T(8,128)(2,1)} %copy-done.2), calls=%async_computation | async-start | bytes 2621440 | tf_op jit(solution)/shard_map/cond/branch_0_fun/all_to_all | solution.py:335
  72.9 3.4 %slot_pick.7 = (bf16[20,32,128]{2,1,0:T(8,128)(2,1)S(1)}, bf16[20,32,128]{2,1,0:T(8,128)(2,1)}, bf16[20,32,128]{2,1,0:T(8,128)(2,1)}, bf16[20,32,128]{2,1,0:T(8,128)(2,1)S(1)}) custom-call(s32[1]{0:T(128)} %bitcast.after.me, s32[80]{0:T(128)S(1)} %get-tuple-element.1492.first, s32[80]{0:T(128)S(1)} %get-tuple-element.1491.second, ...), custom_call_target="tpu_custom_call" | custom-call | bytes 2097152 | tf_op jit(solution)/shard_map/cond/branch_0_fun/slot_pick/pallas_call | solution.py:197
  76.3 1.6 %collective-permute-start.6 = (bf16[20,32,128]{2,1,0:T(8,128)(2,1)}, bf16[20,32,128]{2,1,0:T(8,128)(2,1)S(1)}, u32[]{:S(2)}, u32[]{:S(2)}) collective-permute-start(bf16[20,32,128]{2,1,0:T(8,128)(2,1)} %get-tuple-element.116), channel_id=1, source_target_pairs={{0,1},{1,2},{2,3},{3,0},{4,5},{5,6},{6,7},{7,4},{8,9},{9,10},{10,1... | collective-permute-start | bytes 491528 | tf_op jit(solution)/shard_map/cond/branch_0_fun/ppermute | solution.py:326
  77.9 2.9 %collective-permute-start.7 = (bf16[20,32,128]{2,1,0:T(8,128)(2,1)}, bf16[20,32,128]{2,1,0:T(8,128)(2,1)S(1)}, u32[]{:S(2)}, u32[]{:S(2)}) collective-permute-start(bf16[20,32,128]{2,1,0:T(8,128)(2,1)} %get-tuple-element.117), channel_id=1, source_target_pairs={{0,2},{1,3},{2,0},{3,1},{4,6},{5,7},{6,4},{7,5},{8,10},{9,11},{10,... | collective-permute-start | bytes 491528 | tf_op jit(solution)/shard_map/cond/branch_0_fun/ppermute | solution.py:326
  82.1 23.2 %all-to-all-done.got = bf16[32,5,32,128]{3,2,1,0:T(8,128)(2,1)} async-done(((bf16[32,5,32,128]{3,2,1,0:T(8,128)(2,1)}), bf16[32,5,32,128]{3,2,1,0:T(8,128)(2,1)}, u32[]{:S(2)}, u32[]{:S(2)}) %all-to-all-start) | async-done | bytes 1310752 | tf_op jit(solution)/shard_map/cond/branch_0_fun/all_to_all | solution.py:335
  105.3 2.7 %slot_pick.6 = (bf16[20,32,128]{2,1,0:T(8,128)(2,1)S(1)}, bf16[20,32,128]{2,1,0:T(8,128)(2,1)S(1)}, bf16[20,32,128]{2,1,0:T(8,128)(2,1)S(1)}, bf16[20,32,128]{2,1,0:T(8,128)(2,1)S(1)}) custom-call(s32[1]{0:T(128)} %bitcast.after.me, s32[80]{0:T(128)S(1)} %get-tuple-element.1492.first, s32[80]{0:T(128)S(1)} %get-tuple-element.1491.second, ...), custom_call_target="tpu_custom_call" | custom-call | bytes 2097152 | tf_op jit(solution)/shard_map/cond/branch_0_fun/slot_pick/pallas_call | solution.py:197
  107.9 1.7 %collective-permute-start.3 = (bf16[20,32,128]{2,1,0:T(8,128)(2,1)S(1)}, bf16[20,32,128]{2,1,0:T(8,128)(2,1)S(1)}, u32[]{:S(2)}, u32[]{:S(2)}) collective-permute-start(bf16[20,32,128]{2,1,0:T(8,128)(2,1)S(1)} %get-tuple-element.112), channel_id=1, source_target_pairs={{0,1},{1,2},{2,3},{3,0},{4,5},{5,6},{6,7},{7,4},{8,9},{9,10},{10,1... | collective-permute-start | bytes 491528 | tf_op jit(solution)/shard_map/cond/branch_0_fun/ppermute | solution.py:326
  109.6 2.9 %collective-permute-start.4 = (bf16[20,32,128]{2,1,0:T(8,128)(2,1)S(1)}, bf16[20,32,128]{2,1,0:T(8,128)(2,1)S(1)}, u32[]{:S(2)}, u32[]{:S(2)}) collective-permute-start(bf16[20,32,128]{2,1,0:T(8,128)(2,1)S(1)} %get-tuple-element.113), channel_id=1, source_target_pairs={{0,2},{1,3},{2,0},{3,1},{4,6},{5,7},{6,4},{7,5},{8,10},{9,11},{10,... | collective-permute-start | bytes 491528 | tf_op jit(solution)/shard_map/cond/branch_0_fun/ppermute | solution.py:326
  112.5 1.3 %collective-permute-start.5 = (bf16[20,32,128]{2,1,0:T(8,128)(2,1)S(1)}, bf16[20,32,128]{2,1,0:T(8,128)(2,1)S(1)}, u32[]{:S(2)}, u32[]{:S(2)}) collective-permute-start(bf16[20,32,128]{2,1,0:T(8,128)(2,1)S(1)} %get-tuple-element.114), channel_id=1, source_target_pairs={{0,3},{1,0},{2,1},{3,2},{4,7},{5,4},{6,5},{7,6},{8,11},{9,8},{10,9... | collective-permute-start | bytes 491528 | tf_op jit(solution)/shard_map/cond/branch_0_fun/ppermute | solution.py:326
  113.8 3.3 %product0.3.rest_4_ = bf16[2,1,80,128,128]{4,3,2,1,0:T(8,128)(2,1)} custom-call(s32[1]{0:T(128)} %bitcast.after.me, s32[320]{0:T(512)S(1)} %sub.31.pos, bf16[80,128,128]{2,1,0:T(8,128)(2,1)S(1)} %coef_join.3.after.coef, bf16[20,32,128]{2,1,0:T(8,128)(2,1)S(1)} %get-tuple-element.115.rest_0_, bf16[20,32,128]{2,1,0:T(8,128)(2,1)S(1)} %collective-permute-done.6.rest_1_, ...), custom_call_target="tpu_custom_call" | custom-call | flops 335544320 | bytes 6291456 | tf_op jit(solution)/shard_map/cond/branch_0_fun/product0/pallas_call | solution.py:230
  117.8 3.3 %product1.3 = bf16[2,1,80,128,128]{4,3,2,1,0:T(8,128)(2,1)} custom-call(s32[1]{0:T(128)} %bitcast.after.me, s32[320]{0:T(512)S(1)} %sub.31.pos, bf16[80,128,128]{2,1,0:T(8,128)(2,1)S(1)} %coef_join.3.after.coef, bf16[20,32,128]{2,1,0:T(8,128)(2,1)S(1)} %get-tuple-element.111.rest_0_, ...), custom_call_target="tpu_custom_call", output_to_operand_aliasing={{}: (7, {})} | custom-call | flops 335544320 | bytes 6291456 | tf_op jit(solution)/shard_map/cond/branch_0_fun/product1/pallas_call | solution.py:230
  (95 shorter events, 14.1 us)
Async XLA Ops:
  5.9 9.7 %copy-start.6 = (s32[4,4]{1,0:T(4,128)S(1)}, s32[4,4]{1,0:T(4,128)}, u32[]{:S(2)}) copy-start(s32[4,4]{1,0:T(4,128)} %param.12) | copy-start | bytes 196
  5.9 9.7 %copy-start.21 = (s32[320,2]{0,1:T(2,128)S(1)}, s32[320,2]{0,1:T(2,128)}, u32[]{:S(2)}) copy-start(s32[320,2]{0,1:T(2,128)} %param.13) | copy-start | bytes 7684
  9.6 4.3 %collective-permute-start.27 = (bf16[8,4,32,480]{3,2,1,0:T(8,128)(2,1)S(1)}, bf16[8,4,32,480]{3,2,1,0:T(8,128)(2,1)}, u32[]{:S(2)}, u32[]{:S(2)}) collective-permute-start(bf16[8,4,32,480]{3,2,1,0:T(8,128)(2,1)S(1)} %get-tuple-element.180), channel_id=1, source_target_pairs={{0,4},{4,0},{1,5},{5,1},{2,6},{6,2},{3,7},{7,3},{8,12},{12,8},{9,1... | collective-permute-start | bytes 2949128 | tf_op jit(solution)/shard_map/ppermute | solution.py:267
  9.7 4.3 %collective-permute-start.28 = (bf16[8,4,32,480]{3,2,1,0:T(8,128)(2,1)S(1)}, bf16[8,4,32,480]{3,2,1,0:T(8,128)(2,1)}, u32[]{:S(2)}, u32[]{:S(2)}) collective-permute-start(bf16[8,4,32,480]{3,2,1,0:T(8,128)(2,1)S(1)} %get-tuple-element.182), channel_id=1, source_target_pairs={{0,4},{4,0},{1,5},{5,1},{2,6},{6,2},{3,7},{7,3},{8,12},{12,8},{9,1... | collective-permute-start | bytes 2949128 | tf_op jit(solution)/shard_map/ppermute | solution.py:267
  15.7 5.4 %copy-start.18 = (s32[8]{0:T(128)}, s32[8]{0:T(128)S(1)}, u32[]{:S(2)}) copy-start(s32[8]{0:T(128)S(1)} %get-tuple-element.98.listed) | copy-start | bytes 100 | tf_op jit(solution)/shard_map/cond
  21.1 45.9 %all-to-all-start.1 = ((bf16[32,5,32,128]{3,2,1,0:T(8,128)(2,1)}), bf16[32,5,32,128]{3,2,1,0:T(8,128)(2,1)}, u32[]{:S(2)}, u32[]{:S(2)}) async-start(bf16[32,5,32,128]{3,2,1,0:T(8,128)(2,1)} %tile_pick.6.after), calls=%async_computation.1 | async-start | bytes 2621440 | tf_op jit(solution)/shard_map/cond/branch_0_fun/all_to_all | solution.py:335
  35.0 7.3 %collective-permute-start = (bf16[20,32,128]{2,1,0:T(8,128)(2,1)S(1)}, bf16[20,32,128]{2,1,0:T(8,128)(2,1)S(1)}, u32[]{:S(2)}, u32[]{:S(2)}) collective-permute-start(bf16[20,32,128]{2,1,0:T(8,128)(2,1)S(1)} %get-tuple-element.102), channel_id=1, source_target_pairs={{0,1},{1,2},{2,3},{3,0},{4,5},{5,6},{6,7},{7,4},{8,9},{9,10},{10,1... | collective-permute-start | bytes 491528 | tf_op jit(solution)/shard_map/cond/branch_0_fun/ppermute | solution.py:326
  36.7 10.1 %collective-permute-start.1 = (bf16[20,32,128]{2,1,0:T(8,128)(2,1)S(1)}, bf16[20,32,128]{2,1,0:T(8,128)(2,1)S(1)}, u32[]{:S(2)}, u32[]{:S(2)}) collective-permute-start(bf16[20,32,128]{2,1,0:T(8,128)(2,1)S(1)} %get-tuple-element.103), channel_id=1, source_target_pairs={{0,2},{1,3},{2,0},{3,1},{4,6},{5,7},{6,4},{7,5},{8,10},{9,11},{10,... | collective-permute-start | bytes 491528 | tf_op jit(solution)/shard_map/cond/branch_0_fun/ppermute | solution.py:326
  39.6 7.2 %collective-permute-start.2 = (bf16[20,32,128]{2,1,0:T(8,128)(2,1)S(1)}, bf16[20,32,128]{2,1,0:T(8,128)(2,1)S(1)}, u32[]{:S(2)}, u32[]{:S(2)}) collective-permute-start(bf16[20,32,128]{2,1,0:T(8,128)(2,1)S(1)} %get-tuple-element.104), channel_id=1, source_target_pairs={{0,3},{1,0},{2,1},{3,2},{4,7},{5,4},{6,5},{7,6},{8,11},{9,8},{10,9... | collective-permute-start | bytes 491528 | tf_op jit(solution)/shard_map/cond/branch_0_fun/ppermute | solution.py:326
  55.1 1.1 copy-start.2
  56.2 16.4 %copy-start.9 = (s32[80]{0:T(128)S(1)}, s32[80]{0:T(128)}, u32[]{:S(2)}) copy-start(s32[80]{0:T(128)} %get-tuple-element.391) | copy-start | bytes 964 | tf_op jit(solution)/shard_map/cond
  56.2 16.4 %copy-start.12 = (s32[80]{0:T(128)S(1)}, s32[80]{0:T(128)}, u32[]{:S(2)}) copy-start(s32[80]{0:T(128)} %get-tuple-element.379) | copy-start | bytes 964 | tf_op jit(solution)/shard_map/cond
  56.2 16.4 %copy-start.15 = (s32[80]{0:T(128)S(1)}, s32[80]{0:T(128)}, u32[]{:S(2)}) copy-start(s32[80]{0:T(128)} %get-tuple-element.1574) | copy-start | bytes 964 | tf_op jit(solution)/shard_map/cond
  56.2 16.4 %copy-start.22 = (pred[80]{0:T(512)(128)(4,1)S(1)}, pred[80]{0:T(512)(128)(4,1)}, u32[]{:S(2)}) copy-start(pred[80]{0:T(512)(128)(4,1)} %get-tuple-element.424) | copy-start | bytes 244 | tf_op jit(solution)/shard_map/cond
  56.2 16.4 %copy-start.25 = (pred[80]{0:T(512)(128)(4,1)S(1)}, pred[80]{0:T(512)(128)(4,1)}, u32[]{:S(2)}) copy-start(pred[80]{0:T(512)(128)(4,1)} %get-tuple-element.415) | copy-start | bytes 244 | tf_op jit(solution)/shard_map/cond
  56.2 16.4 %copy-start.28 = (s32[80]{0:T(128)S(1)}, s32[80]{0:T(128)}, u32[]{:S(2)}) copy-start(s32[80]{0:T(128)} %get-tuple-element.1577) | copy-start | bytes 964 | tf_op jit(solution)/shard_map/cond
  56.2 16.4 %copy-start.31 = (s32[80]{0:T(128)S(1)}, s32[80]{0:T(128)}, u32[]{:S(2)}) copy-start(s32[80]{0:T(128)} %get-tuple-element.1580) | copy-start | bytes 964 | tf_op jit(solution)/shard_map/cond
  67.0 38.3 %all-to-all-start = ((bf16[32,5,32,128]{3,2,1,0:T(8,128)(2,1)}), bf16[32,5,32,128]{3,2,1,0:T(8,128)(2,1)}, u32[]{:S(2)}, u32[]{:S(2)}) async-start(bf16[32,5,32,128]{3,2,1,0:T(8,128)(2,1)} %copy-done.2), calls=%async_computation | async-start | bytes 2621440 | tf_op jit(solution)/shard_map/cond/branch_0_fun/all_to_all | solution.py:335
  76.3 36.2 %collective-permute-start.6 = (bf16[20,32,128]{2,1,0:T(8,128)(2,1)}, bf16[20,32,128]{2,1,0:T(8,128)(2,1)S(1)}, u32[]{:S(2)}, u32[]{:S(2)}) collective-permute-start(bf16[20,32,128]{2,1,0:T(8,128)(2,1)} %get-tuple-element.116), channel_id=1, source_target_pairs={{0,1},{1,2},{2,3},{3,0},{4,5},{5,6},{6,7},{7,4},{8,9},{9,10},{10,1... | collective-permute-start | bytes 491528 | tf_op jit(solution)/shard_map/cond/branch_0_fun/ppermute | solution.py:326
  77.9 36.0 %collective-permute-start.7 = (bf16[20,32,128]{2,1,0:T(8,128)(2,1)}, bf16[20,32,128]{2,1,0:T(8,128)(2,1)S(1)}, u32[]{:S(2)}, u32[]{:S(2)}) collective-permute-start(bf16[20,32,128]{2,1,0:T(8,128)(2,1)} %get-tuple-element.117), channel_id=1, source_target_pairs={{0,2},{1,3},{2,0},{3,1},{4,6},{5,7},{6,4},{7,5},{8,10},{9,11},{10,... | collective-permute-start | bytes 491528 | tf_op jit(solution)/shard_map/cond/branch_0_fun/ppermute | solution.py:326
  80.8 33.1 %collective-permute-start.8 = (bf16[20,32,128]{2,1,0:T(8,128)(2,1)S(1)}, bf16[20,32,128]{2,1,0:T(8,128)(2,1)S(1)}, u32[]{:S(2)}, u32[]{:S(2)}) collective-permute-start(bf16[20,32,128]{2,1,0:T(8,128)(2,1)S(1)} %get-tuple-element.118), channel_id=1, source_target_pairs={{0,3},{1,0},{2,1},{3,2},{4,7},{5,4},{6,5},{7,6},{8,11},{9,8},{10,9... | collective-permute-start | bytes 491528 | tf_op jit(solution)/shard_map/cond/branch_0_fun/ppermute | solution.py:326
  107.9 9.3 %collective-permute-start.3 = (bf16[20,32,128]{2,1,0:T(8,128)(2,1)S(1)}, bf16[20,32,128]{2,1,0:T(8,128)(2,1)S(1)}, u32[]{:S(2)}, u32[]{:S(2)}) collective-permute-start(bf16[20,32,128]{2,1,0:T(8,128)(2,1)S(1)} %get-tuple-element.112), channel_id=1, source_target_pairs={{0,1},{1,2},{2,3},{3,0},{4,5},{5,6},{6,7},{7,4},{8,9},{9,10},{10,1... | collective-permute-start | bytes 491528 | tf_op jit(solution)/shard_map/cond/branch_0_fun/ppermute | solution.py:326
  109.6 7.9 %collective-permute-start.4 = (bf16[20,32,128]{2,1,0:T(8,128)(2,1)S(1)}, bf16[20,32,128]{2,1,0:T(8,128)(2,1)S(1)}, u32[]{:S(2)}, u32[]{:S(2)}) collective-permute-start(bf16[20,32,128]{2,1,0:T(8,128)(2,1)S(1)} %get-tuple-element.113), channel_id=1, source_target_pairs={{0,2},{1,3},{2,0},{3,1},{4,6},{5,7},{6,4},{7,5},{8,10},{9,11},{10,... | collective-permute-start | bytes 491528 | tf_op jit(solution)/shard_map/cond/branch_0_fun/ppermute | solution.py:326
  112.5 5.3 %collective-permute-start.5 = (bf16[20,32,128]{2,1,0:T(8,128)(2,1)S(1)}, bf16[20,32,128]{2,1,0:T(8,128)(2,1)S(1)}, u32[]{:S(2)}, u32[]{:S(2)}) collective-permute-start(bf16[20,32,128]{2,1,0:T(8,128)(2,1)S(1)} %get-tuple-element.114), channel_id=1, source_target_pairs={{0,3},{1,0},{2,1},{3,2},{4,7},{5,4},{6,5},{7,6},{8,11},{9,8},{10,9... | collective-permute-start | bytes 491528 | tf_op jit(solution)/shard_map/cond/branch_0_fun/ppermute | solution.py:326
